TPU v7x, 32 devices: a whole 2x2x4 slice. The times are simulated.
32 devices in a mesh: segment: 2 (over core), seq: 8 (over z, x), head: 2 (over y).
Axes of the slice: x: 2, y: 2, z: 4, core: 2. Of those that a mesh axis runs over, the one named last changes fastest.
Arguments:
- stream_in: bfloat16 [2, 2048, 3072], P('segment', 'seq'), may hold values from -6 to 6
- queries: bfloat16 [2, 2048, 1536], P('segment', 'seq', 'head'), may hold values from -8 to 8
- keys: bfloat16 [2, 2048, 1536], P('segment', 'seq', 'head'), may hold values from -8 to 8
- values: bfloat16 [2, 2048, 1536], P('segment', 'seq', 'head'), may hold values from -6 to 6
- out_weight: bfloat16 [2, 1536, 3072], P('segment', 'head'), may hold values from -0.15625 to 0.15625
- gate_scale: float32 [2, 3072], P('segment'), may hold values from 0.5 to 2
Outputs:
- stream_out: bfloat16 [2, 2048, 3072], P('segment', 'seq', 'head')
All inputs are finite; a program needn't handle non-finite values.
Results may differ from a plain program's by a relative error of at most 0.0065.
Values may be sent and summed in bfloat16 or wider, within the bound.
No kernel may reach another device: no remote copies, remote signals or barrier semaphores. Data moves between devices by JAX's collectives and lax.ppermute only.
A program may use at most 64 MiB of HBM per device.

v0:
```python
import functools
import math

import jax
import jax.numpy as jnp
from jax import lax
from jax.experimental import pallas as pl
from jax.experimental.pallas import tpu as pltpu
from jax.sharding import PartitionSpec as P


HD = 128
STATE = HD + 16
SHARED = 64
LOG2E = 1.4426950408889634
VMEM = pl.BlockSpec(memory_space=pltpu.VMEM)


def limit(mib):
    return pltpu.CompilerParams(vmem_limit_bytes=mib << 20)


def pack_kernel(groups, local, cols, spot_ref, k_any, v_any, q_any, w_any, *rest):
    outs, (k_ref, v_ref, q_ref, sems) = rest[:-4], rest[-4:]
    mine_role = spot_ref[0]
    lanes = pl.ds(pl.multiple_of(spot_ref[1] * cols, HD), cols)
    third = w_any.at[pl.ds(pl.multiple_of((mine_role * local + 2) * HD, HD), HD), lanes]
    start = w_any.at[pl.ds(pl.multiple_of(mine_role * local * HD, HD), SHARED), lanes]
    loads = [
        pltpu.make_async_copy(source, target, sems.at[at])
        for at, (source, target) in enumerate(
            (
                (k_any, k_ref),
                (v_any, v_ref),
                (q_any, q_ref),
                (third, outs[-1].at[:HD, :]),
                (start, outs[-1].at[HD:, :]),
            )
        )
    ]
    for load in loads:
        load.start()
    rows, width = k_ref.shape
    half = width // 2
    loads[0].wait()
    loads[1].wait()
    for side in range(2):
        role = mine_role if side == 0 else 1 - mine_role
        for heads, out in zip(groups, outs[side * len(groups) :]):
            for place, head in enumerate(heads):
                lanes = pl.ds(pl.multiple_of(role * half + head * HD, HD), HD)
                base = place * 2 * HD
                for piece in range(rows // HD):
                    out[base : base + HD, piece * HD : (piece + 1) * HD] = k_ref[
                        piece * HD : (piece + 1) * HD, lanes
                    ]
                out[base + HD : base + 2 * HD, :] = v_ref[:, lanes].T
    loads[2].wait()
    for side in range(2):
        role = mine_role if side == 0 else 1 - mine_role
        for head in range(half // HD):
            lanes = pl.ds(pl.multiple_of(role * half + head * HD, HD), HD)
            outs[side - 3][head * HD : (head + 1) * HD, :] = q_ref[:, lanes].T
    loads[3].wait()
    loads[4].wait()


SMEM = pl.BlockSpec(memory_space=pltpu.SMEM)
ANY = pl.BlockSpec(memory_space=pl.ANY)


def in_hbm(x):
    return pltpu.with_memory_space_constraint(x, pltpu.HBM)


def pack(spot, keys, values, queries, weight, groups, cols):
    rows, width = keys.shape
    shapes = [
        jax.ShapeDtypeStruct((len(heads) * 2 * HD, rows), jnp.bfloat16) for heads in groups
    ]
    asked = jax.ShapeDtypeStruct((width // 2, rows), jnp.bfloat16)
    third = jax.ShapeDtypeStruct((HD + SHARED, cols), jnp.bfloat16)
    return pl.pallas_call(
        functools.partial(pack_kernel, groups, width // 2 // HD, cols),
        out_shape=tuple(shapes + shapes + [asked, asked, third]),
        in_specs=[SMEM, ANY, ANY, ANY, ANY],
        out_specs=(VMEM,) * (2 * len(groups) + 3),
        scratch_shapes=[pltpu.VMEM((rows, width), jnp.bfloat16)] * 3
        + [pltpu.SemaphoreType.DMA((5,))],
        compiler_params=limit(8),
        name="pack",
    )(spot, in_hbm(keys), in_hbm(values), in_hbm(queries), in_hbm(weight))


def carve_kernel(local, cols, parts, spot_ref, w_any, *rest):
    out, sems = rest
    lanes = pl.ds(pl.multiple_of(spot_ref[1] * cols, HD), cols)
    unit = HD // 2
    copies, to = [], 0
    for ours, first, count in parts:
        role = spot_ref[0] if ours else 1 - spot_ref[0]
        for at in range(first, first + count, unit):
            row = pl.multiple_of(role * local * HD + at, unit)
            copies.append(
                pltpu.make_async_copy(
                    w_any.at[pl.ds(row, unit), lanes],
                    out.at[to : to + unit, :],
                    sems.at[len(copies)],
                )
            )
            to += unit
    for copy in copies:
        copy.start()
    for copy in copies:
        copy.wait()


def carve(spot, weight, local, cols, parts):
    rows = sum(part[2] for part in parts)
    return pl.pallas_call(
        functools.partial(carve_kernel, local, cols, parts),
        out_shape=jax.ShapeDtypeStruct((rows, cols), weight.dtype),
        in_specs=[SMEM, ANY],
        out_specs=VMEM,
        scratch_shapes=[pltpu.SemaphoreType.DMA((rows // (HD // 2),))],
        compiler_params=limit(4),
        name="carve",
    )(spot, in_hbm(weight))


def absorb_kernel(heads, count, first, last, *refs):
    q_refs, kv_refs, rest = refs[:2], refs[2 : 2 + count], refs[2 + count :]
    state = None if first else rest[0]
    outs = rest if first else rest[1:]
    keys = kv_refs[0].shape[1]
    factor = LOG2E / math.sqrt(HD)
    for place, head in enumerate(heads):
        base = place * 2 * HD
        key = jnp.concatenate(
            [
                kv[base : base + HD, piece * HD : (piece + 1) * HD]
                for kv in kv_refs
                for piece in range(keys // HD)
            ],
            axis=0,
        )
        value = jnp.concatenate([kv[base + HD : base + 2 * HD, :] for kv in kv_refs], axis=1)
        tall = jnp.concatenate([value, jnp.ones((16, value.shape[1]), jnp.bfloat16)], axis=0)
        for side, q_ref in enumerate(q_refs):
            query = q_ref[head * HD : (head + 1) * HD, :]
            scores = jnp.dot(key, query, preferred_element_type=jnp.float32)
            top = jnp.max(scores, axis=0, keepdims=True)
            if not first:
                top_old = state[place, side, HD + 8 : HD + 9, :]
                top = jnp.maximum(top_old, top)
            raised = jnp.exp2((scores - top) * factor).astype(jnp.bfloat16)
            both = jnp.dot(tall, raised, preferred_element_type=jnp.float32)
            mixed, total = both[:HD], both[HD : HD + 8]
            if not first:
                shrink = jnp.exp2((top_old - top) * factor)
                mixed = state[place, side, :HD, :] * shrink + mixed
                total = state[place, side, HD : HD + 8, :] * shrink + total
            if last:
                done = mixed * (1.0 / total[:1])
                outs[side][:, place * HD : (place + 1) * HD] = done.T.astype(jnp.bfloat16)
            else:
                outs[0][place, side, :HD, :] = mixed
                outs[0][place, side, HD : HD + 8, :] = total
                outs[0][place, side, HD + 8 :, :] = jnp.broadcast_to(top, total.shape)


def absorb(asking, blocks, heads, state, last):
    rows = asking[0].shape[1]
    keys = blocks[0].shape[1] * len(blocks)
    count = len(heads)
    first = state is None
    if last:
        shape = jax.ShapeDtypeStruct((rows, count * HD), jnp.bfloat16)
        out_shape, out_specs = (shape, shape), (VMEM, VMEM)
    else:
        out_shape = jax.ShapeDtypeStruct((count, 2, STATE, rows), jnp.float32)
        out_specs = VMEM
    operands = [*asking, *blocks] + ([] if first else [state])
    return pl.pallas_call(
        functools.partial(absorb_kernel, heads, len(blocks), first, last),
        out_shape=out_shape,
        in_specs=[VMEM] * len(operands),
        out_specs=out_specs,
        input_output_aliases={} if first or last else {len(operands) - 1: 0},
        cost_estimate=pl.CostEstimate(
            flops=8 * count * rows * keys * HD,
            bytes_accessed=count * rows * HD * 12,
            transcendentals=2 * count * rows * keys,
        ),
        compiler_params=limit(12),
        name="absorb",
    )(*operands)


def base_kernel(wide, spot_ref, ours, third, back, weight, stream, gate, out, kept):
    left = jnp.concatenate([ours[...], third[...], back[...]], axis=1)
    depth = left.shape[1]
    cols = out.shape[1]
    for at in range(cols // wide):
        lanes = slice(at * wide, (at + 1) * wide)
        scale = gate[:, pl.ds(pl.multiple_of(spot_ref[1] * cols + at * wide, HD), wide)]
        branch = jnp.dot(left, weight[:depth, lanes], preferred_element_type=jnp.float32)
        out[:, lanes] = stream[:, lanes].astype(jnp.float32) + scale * branch
        kept[:, lanes] = scale


def first_base(spot, ours, third, back, weight, stream, gate, wide):
    rows, cols = stream.shape
    return pl.pallas_call(
        functools.partial(base_kernel, wide),
        out_shape=(
            jax.ShapeDtypeStruct((rows, cols), jnp.float32),
            jax.ShapeDtypeStruct((1, cols), gate.dtype),
        ),
        in_specs=[SMEM] + [VMEM] * 6,
        out_specs=(VMEM, VMEM),
        cost_estimate=pl.CostEstimate(
            flops=10 * HD * rows * cols, bytes_accessed=rows * cols * 4, transcendentals=0
        ),
        compiler_params=limit(12),
        name="first_base",
    )(spot, ours, third, back, weight, stream, gate)


def middle_kernel(wide, over, cross, passed, relayed, others, base, gate, out):
    left = jnp.concatenate([over[...], cross[...]], axis=1)
    half = others.shape[0] // 2
    for at in range(base.shape[1] // wide):
        lanes = slice(at * wide, (at + 1) * wide)
        right = jnp.concatenate(
            [
                passed[HD:, lanes],
                others[:half, lanes],
                relayed[HD:, lanes],
                others[half:, lanes],
            ],
            axis=0,
        )
        branch = jnp.dot(left, right, preferred_element_type=jnp.float32)
        out[:, lanes] = base[:, lanes] + gate[:, lanes] * branch


def middle(over, cross, passed, relayed, others, base, gate, wide):
    return pl.pallas_call(
        functools.partial(middle_kernel, wide),
        out_shape=jax.ShapeDtypeStruct(base.shape, jnp.float32),
        in_specs=[VMEM] * 7,
        out_specs=VMEM,
        input_output_aliases={5: 0},
        cost_estimate=pl.CostEstimate(
            flops=8 * HD * base.size, bytes_accessed=base.size, transcendentals=0
        ),
        compiler_params=limit(12),
        name="middle",
    )(over, cross, passed, relayed, others, base, gate)


def finish_kernel(pieces, wide, *refs):
    lefts, rights = refs[:pieces], refs[pieces : 2 * pieces]
    base, gate, out, held, sems = refs[2 * pieces :]
    left = jnp.concatenate([ref[...] for ref in lefts], axis=1)
    copies = []
    for at in range(base.shape[1] // wide):
        lanes = slice(at * wide, (at + 1) * wide)
        right = jnp.concatenate(
            [rights[0][-HD:, lanes]] + [ref[:HD, lanes] for ref in rights[1:]], axis=0
        )
        branch = jnp.dot(left, right, preferred_element_type=jnp.float32)
        held[:, lanes] = (base[:, lanes] + gate[:, lanes] * branch).astype(held.dtype)
        copies.append(pltpu.make_async_copy(held.at[:, lanes], out.at[:, lanes], sems.at[at]))
        copies[-1].start()
    for copy in copies:
        copy.wait()


def finish(pieces, weights, base, gate, wide):
    operands = [*pieces, *weights, base, gate]
    return pl.pallas_call(
        functools.partial(finish_kernel, len(pieces), wide),
        out_shape=jax.ShapeDtypeStruct(base.shape, jnp.bfloat16),
        in_specs=[VMEM] * len(operands),
        out_specs=ANY,
        scratch_shapes=[
            pltpu.VMEM(base.shape, jnp.bfloat16),
            pltpu.SemaphoreType.DMA((base.shape[1] // wide,)),
        ],
        cost_estimate=pl.CostEstimate(
            flops=2 * len(pieces) * HD * base.size, bytes_accessed=base.size * 2, transcendentals=0
        ),
        compiler_params=limit(12),
        name="finish",
    )(*operands)


def role_of(member):
    return member // 2 % 2


def per_device(stream_in, queries, keys, values, out_weight, gate_scale):
    sections = lax.axis_size("segment")
    seq_count = lax.axis_size("seq")
    shares = lax.axis_size("head")
    local = queries.shape[2] // HD // 2
    cycle_len = min(32, seq_count)
    stride = seq_count // cycle_len
    planes = cycle_len // 2
    rounds = planes // 2

    partner = {m: m ^ 2 for m in range(cycle_len)}
    beside = {m: m ^ 1 for m in range(cycle_len)}
    beyond = {}
    for role in range(2):
        for column in range(2):
            line = [p * 2 + column for p in range(planes) if role_of(p * 2) == role]
            for at, m in enumerate(line):
                beyond[m] = line[(at + 1) % len(line)]

    def hop(block, towards, shift=0, by=0):
        pairs = []
        for section in range(sections):
            for member in range(cycle_len):
                for video in range(stride):
                    for share in range(shares):
                        origin = section * seq_count + member * stride + video
                        target = (
                            (section + shift) % sections * seq_count
                            + towards[member] * stride
                            + video
                        )
                        pairs.append(
                            (origin * shares + share, target * shares + (share + by) % shares)
                        )
        return lax.ppermute(block, ("segment", "seq", "head"), pairs)

    still = {m: m for m in range(cycle_len)}
    share = lax.axis_index("head").astype(jnp.int32)
    role = role_of(lax.axis_index("seq").astype(jnp.int32) // stride)
    groups = [(0, 1), (2,)]

    col_count = out_weight.shape[2] // shares
    spots = {by: jnp.stack([role, lax.rem(share + by, shares)]) for by in range(1, shares)}
    packed = pack(
        spots[1], keys[0], values[0], queries[0], out_weight[0], groups, col_count
    )
    mine, give = packed[: len(groups)], packed[len(groups) : 2 * len(groups)]
    my_query, give_query, own_thirds = packed[-3:]
    got = [None] * len(groups)
    far = [[None] * 2 for _ in groups]
    near = [[None] * 2 for _ in groups]
    own = [None] * len(groups)
    everyone = range(len(groups))
    for g in everyone:
        got[g] = hop(give[g], partner, 1)
        far[g][0] = hop(mine[g], beyond, 1)
        near[g][0] = hop(mine[g], beside, 1)
        own[g] = hop(mine[g], still, 1)
    asking = [hop(my_query, still, 1), hop(give_query, partner, 1)]

    lent = {}
    rest = 2 * HD - SHARED
    for by in range(1, shares):
        part = own_thirds
        if by > 1:
            wanted = ((True, 2 * HD, HD), (True, 0, SHARED))
            part = carve(spots[by], out_weight[0], local, col_count, wanted)
        passed = hop(part, still, 1, by)
        wanted = ((True, SHARED, rest), (False, SHARED, rest))
        part = carve(spots[by], out_weight[0], local, col_count, wanted)
        lent[by] = (passed, hop(passed, partner), hop(part, still, 1, by))
    here = jnp.stack([role, share])
    kept = carve(
        here, out_weight[0], local, col_count, ((True, 0, local * HD), (False, 0, local * HD))
    )
    lines = carve(
        here * jnp.array([0, 1], jnp.int32),
        stream_in[0],
        local,
        col_count,
        ((True, 0, stream_in.shape[1]),),
    )
    weight = hop(kept, still, 1)
    stream = hop(lines, still, 1)
    gate = hop(gate_scale, still, 1)

    def fold(g, blocks, held, last=False):
        return absorb(asking, blocks, groups[g], held, last)

    attended = []
    for g in everyone:
        far[g][1] = hop(got[g], beyond)
        near[g][1] = hop(got[g], beside)
        state = fold(g, [own[g], got[g], *near[g]], None)
        arrived = far[g]
        for turn in range(1, rounds):
            onward = [hop(arrived[i], beside) for i in range(2)]
            state = fold(g, [arrived[0], onward[0]], state)
            state = fold(g, arrived[1:], state)
            if turn < rounds - 1:
                state = fold(g, onward[1:], state)
                arrived = [hop(arrived[i], beyond) for i in range(2)]
            else:
                attended.append(fold(g, onward[1:], state, True))

    home = []
    for g in everyone:
        ours, theirs = attended[g]
        back = hop(theirs, partner)
        over = {by: hop(ours, still, 0, by) for by in range(1, shares)}
        cross = {by: hop(theirs, partner, 0, by) for by in range(1, shares)}
        home.append((ours, back, over, cross))

    first, second = home
    base, own_gate = first_base(
        here, first[0], second[0], first[1], weight, stream, gate, 512
    )
    last_pieces, last_weights = [second[1]], [weight]
    for by in range(1, shares):
        passed, relayed, others = lent[by]
        base = middle(
            first[2][by], first[3][by], passed, relayed, others, base, own_gate, 512
        )
        last_pieces += [second[2][by], second[3][by]]
        last_weights += [passed, relayed]
    return finish(last_pieces, last_weights, base, own_gate, 384)[None]


def solution(mesh):
    return jax.shard_map(
        per_device,
        mesh=mesh,
        in_specs=(
            P("segment", "seq", None),
            P("segment", "seq", "head"),
            P("segment", "seq", "head"),
            P("segment", "seq", "head"),
            P("segment", "head", None),
            P("segment", None),
        ),
        out_specs=P("segment", "seq", "head"),
        check_vma=False,
    )
```

profile of v0, /device:TPU:0, one launch (start us, length us, event | category | flops | bytes accessed | tf_op | source)
XLA Modules:
  0.0 106.4 jit_solution(13169546465907371079)
XLA Ops:
  0.1 3.8 %carve.3 = bf16[768,1536]{1,0:T(8,128)(2,1)} custom-call(s32[2]{0:T(128)S(1)} %get-tuple-element.32.spot_ref, bf16[768,3072]{1,0:T(8,128)(2,1)} %bitcast.9), custom_call_target="tpu_custom_call" | custom-call | tf_op jit(solution)/shard_map/carve/pallas_call | solution.py:120
  3.9 0.6 collective-permute-start.13
  4.5 2.0 %pack.1 = (bf16[512,256]{1,0:T(8,128)(2,1)S(1)}, bf16[256,256]{1,0:T(8,128)(2,1)S(1)}, bf16[512,256]{1,0:T(8,128)(2,1)S(1)}, bf16[256,256]{1,0:T(8,128)(2,1)S(1)...) custom-call(s32[2]{0:T(128)S(1)} %pad_add_fusion.spot_ref, ...), custom_call_target="tpu_custom_call" | custom-call | tf_op jit(solution)/shard_map/pack/pallas_call | solution.py:83
  6.5 2.7 %collective-permute-start.2 = (bf16[256,256]{1,0:T(8,128)(2,1)S(1)}, bf16[256,256]{1,0:T(8,128)(2,1)S(1)}, u32[]{:S(2)}, u32[]{:S(2)}) collective-permute-start(bf16[256,256]{1,0:T(8,128)(2,1)S(1)} %get-tuple-element.20), channel_id=1, source_target_pairs={{0,20},{1,21},{2,22},{3,23},{4,16},{5,17},{6,18},{7,19},{8,28},{9,... | collective-permute-start | bytes 393224 | tf_op jit(solution)/shard_map/ppermute | solution.py:338
  9.8 1.2 %collective-permute-done.29.gate = f32[1,3072]{1,0:T(1,128)S(1)} collective-permute-done((f32[1,3072]{1,0:T(1,128)S(1)}, f32[1,3072]{1,0:T(1,128)S(1)}, u32[]{:S(2)}, u32[]{:S(2)}) %collective-permute-start.29) | collective-permute-done | bytes 12320 | tf_op jit(solution)/shard_map/ppermute | solution.py:338
  10.9 1.4 %collective-permute-start.8 = (bf16[256,256]{1,0:T(8,128)(2,1)S(1)}, bf16[256,256]{1,0:T(8,128)(2,1)S(1)}, u32[]{:S(2)}, u32[]{:S(2)}) collective-permute-start(bf16[256,256]{1,0:T(8,128)(2,1)S(1)} %get-tuple-element.21), channel_id=1, source_target_pairs={{0,18},{1,19},{2,16},{3,17},{4,22},{5,23},{6,20},{7,21},{8,26},{9,... | collective-permute-start | bytes 393224 | tf_op jit(solution)/shard_map/ppermute | solution.py:338
  12.3 0.8 collective-permute-done.2.refs_3_
  13.1 2.3 %collective-permute-start.5 = (bf16[256,256]{1,0:T(8,128)(2,1)S(1)}, bf16[256,256]{1,0:T(8,128)(2,1)S(1)}, u32[]{:S(2)}, u32[]{:S(2)}) collective-permute-start(bf16[256,256]{1,0:T(8,128)(2,1)S(1)} %get-tuple-element.21), channel_id=1, source_target_pairs={{0,24},{1,25},{2,26},{3,27},{4,28},{5,29},{6,30},{7,31},{8,16},{9,... | collective-permute-start | bytes 393224 | tf_op jit(solution)/shard_map/ppermute | solution.py:338
  15.4 1.2 %collective-permute-start.1 = (bf16[384,256]{1,0:T(8,128)(2,1)S(1)}, bf16[384,256]{1,0:T(8,128)(2,1)S(1)}, u32[]{:S(2)}, u32[]{:S(2)}) collective-permute-start(bf16[384,256]{1,0:T(8,128)(2,1)S(1)} %get-tuple-element.19), channel_id=1, source_target_pairs={{0,20},{1,21},{2,22},{3,23},{4,16},{5,17},{6,18},{7,19},{8,28},{9,... | collective-permute-start | bytes 589832 | tf_op jit(solution)/shard_map/ppermute | solution.py:338
  16.6 0.8 collective-permute-start.16
  17.4 5.0 %collective-permute-done.5.refs_2_ = bf16[256,256]{1,0:T(8,128)(2,1)S(1)} collective-permute-done((bf16[256,256]{1,0:T(8,128)(2,1)S(1)}, bf16[256,256]{1,0:T(8,128)(2,1)S(1)}, u32[]{:S(2)}, u32[]{:S(2)}) %collective-permute-start.5) | collective-permute-done | bytes 131104 | tf_op jit(solution)/shard_map/ppermute | solution.py:338
  22.5 0.8 collective-permute-start.22
  23.3 1.1 %collective-permute-done.1.refs_1_ = bf16[384,256]{1,0:T(8,128)(2,1)S(1)} collective-permute-done((bf16[384,256]{1,0:T(8,128)(2,1)S(1)}, bf16[384,256]{1,0:T(8,128)(2,1)S(1)}, u32[]{:S(2)}, u32[]{:S(2)}) %collective-permute-start.1) | collective-permute-done | bytes 196640 | tf_op jit(solution)/shard_map/ppermute | solution.py:338
  24.5 1.2 %collective-permute-start.19 = (bf16[512,256]{1,0:T(8,128)(2,1)S(1)}, bf16[512,256]{1,0:T(8,128)(2,1)S(1)}, u32[]{:S(2)}, u32[]{:S(2)}) collective-permute-start(bf16[512,256]{1,0:T(8,128)(2,1)S(1)} %get-tuple-element.26), channel_id=1, source_target_pairs={{0,24},{1,25},{2,26},{3,27},{4,28},{5,29},{6,30},{7,31},{8,16},{9,... | collective-permute-start | bytes 786440 | tf_op jit(solution)/shard_map/ppermute | solution.py:338
  25.6 6.5 %collective-permute-done.16.refs_3_ = bf16[512,256]{1,0:T(8,128)(2,1)S(1)} collective-permute-done((bf16[512,256]{1,0:T(8,128)(2,1)S(1)}, bf16[512,256]{1,0:T(8,128)(2,1)S(1)}, u32[]{:S(2)}, u32[]{:S(2)}) %collective-permute-start.16) | collective-permute-done | bytes 262176 | tf_op jit(solution)/shard_map/ppermute | solution.py:338
  32.1 1.5 %collective-permute-start.9 = (bf16[256,256]{1,0:T(8,128)(2,1)S(1)}, bf16[256,256]{1,0:T(8,128)(2,1)S(1)}, u32[]{:S(2)}, u32[]{:S(2)}) collective-permute-start(bf16[256,256]{1,0:T(8,128)(2,1)S(1)} %collective-permute-done.2.refs_3_), channel_id=1, source_target_pairs={{0,2},{1,3},{2,0},{3,1},{4,6},{5,7},{6,4},{7,5},{8,10},{9,11},{10,... | collective-permute-start | bytes 393224 | tf_op jit(solution)/shard_map/ppermute | solution.py:338
  33.6 0.5 collective-permute-start.6
  34.4 7.3 %collective-permute-done.19.refs_2_ = bf16[512,256]{1,0:T(8,128)(2,1)S(1)} collective-permute-done((bf16[512,256]{1,0:T(8,128)(2,1)S(1)}, bf16[512,256]{1,0:T(8,128)(2,1)S(1)}, u32[]{:S(2)}, u32[]{:S(2)}) %collective-permute-start.19) | collective-permute-done | bytes 262176 | tf_op jit(solution)/shard_map/ppermute | solution.py:338
  41.7 1.1 %collective-permute-start.23 = (bf16[512,256]{1,0:T(8,128)(2,1)S(1)}, bf16[512,256]{1,0:T(8,128)(2,1)S(1)}, u32[]{:S(2)}, u32[]{:S(2)}) collective-permute-start(bf16[512,256]{1,0:T(8,128)(2,1)S(1)} %collective-permute-done.16.refs_3_), channel_id=1, source_target_pairs={{0,2},{1,3},{2,0},{3,1},{4,6},{5,7},{6,4},{7,5},{8,10},{9,11},{10,... | collective-permute-start | bytes 786440 | tf_op jit(solution)/shard_map/ppermute | solution.py:338
  42.9 0.9 collective-permute-start.20
  43.8 1.4 %collective-permute-start.14 = (bf16[192,1536]{1,0:T(8,128)(2,1)S(1)}, bf16[192,1536]{1,0:T(8,128)(2,1)S(1)}, u32[]{:S(2)}, u32[]{:S(2)}) collective-permute-start(bf16[192,1536]{1,0:T(8,128)(2,1)S(1)} %get-tuple-element.24), channel_id=1, source_target_pairs={{0,17},{1,16},{2,19},{3,18},{4,21},{5,20},{6,23},{7,22},{8,25},{9,... | collective-permute-start | bytes 1769480 | tf_op jit(solution)/shard_map/ppermute | solution.py:338
  45.2 1.9 %carve.4 = bf16[384,1536]{1,0:T(8,128)(2,1)S(1)} custom-call(s32[2]{0:T(128)S(1)} %pad_add_fusion.spot_ref, bf16[768,3072]{1,0:T(8,128)(2,1)} %bitcast.11), custom_call_target="tpu_custom_call" | custom-call | tf_op jit(solution)/shard_map/carve/pallas_call | solution.py:120
  47.5 1.8 %carve.5 = bf16[256,1536]{1,0:T(8,128)(2,1)S(1)} custom-call(s32[2]{0:T(128)S(1)} %get-tuple-element.31.spot_ref, bf16[256,3072]{1,0:T(8,128)(2,1)} %bitcast.12), custom_call_target="tpu_custom_call" | custom-call | tf_op jit(solution)/shard_map/carve/pallas_call | solution.py:120
  49.4 1.4 %collective-permute-done.23.refs_5_ = bf16[512,256]{1,0:T(8,128)(2,1)S(1)} collective-permute-done((bf16[512,256]{1,0:T(8,128)(2,1)S(1)}, bf16[512,256]{1,0:T(8,128)(2,1)S(1)}, u32[]{:S(2)}, u32[]{:S(2)}) %collective-permute-start.23) | collective-permute-done | bytes 262176 | tf_op jit(solution)/shard_map/ppermute | solution.py:338
  50.7 0.5 collective-permute-start.28
  51.3 5.1 %collective-permute-done.20.refs_3_ = bf16[512,256]{1,0:T(8,128)(2,1)S(1)} collective-permute-done((bf16[512,256]{1,0:T(8,128)(2,1)S(1)}, bf16[512,256]{1,0:T(8,128)(2,1)S(1)}, u32[]{:S(2)}, u32[]{:S(2)}) %collective-permute-start.20) | collective-permute-done | bytes 262176 | tf_op jit(solution)/shard_map/ppermute | solution.py:338
  56.3 14.4 %collective-permute-done.17.refs_2_ = bf16[512,256]{1,0:T(8,128)(2,1)S(1)} collective-permute-done((bf16[512,256]{1,0:T(8,128)(2,1)S(1)}, bf16[512,256]{1,0:T(8,128)(2,1)S(1)}, u32[]{:S(2)}, u32[]{:S(2)}) %collective-permute-start.17) | collective-permute-done | bytes 262176 | tf_op jit(solution)/shard_map/ppermute | solution.py:338
  70.7 1.5 %collective-permute-start.18 = (bf16[512,256]{1,0:T(8,128)(2,1)S(1)}, bf16[512,256]{1,0:T(8,128)(2,1)S(1)}, u32[]{:S(2)}, u32[]{:S(2)}) collective-permute-start(bf16[512,256]{1,0:T(8,128)(2,1)S(1)} %collective-permute-done.17.refs_2_), channel_id=1, source_target_pairs={{0,2},{1,3},{2,0},{3,1},{4,6},{5,7},{6,4},{7,5},{8,10},{9,11},{10,... | collective-permute-start | bytes 786440 | tf_op jit(solution)/shard_map/ppermute | solution.py:338
  72.2 6.8 %collective-permute-done.18.refs_2_ = bf16[512,256]{1,0:T(8,128)(2,1)S(1)} collective-permute-done((bf16[512,256]{1,0:T(8,128)(2,1)S(1)}, bf16[512,256]{1,0:T(8,128)(2,1)S(1)}, u32[]{:S(2)}, u32[]{:S(2)}) %collective-permute-start.18) | collective-permute-done | bytes 262176 | tf_op jit(solution)/shard_map/ppermute | solution.py:338
  79.0 1.5 %collective-permute-start.4 = (bf16[256,256]{1,0:T(8,128)(2,1)S(1)}, bf16[256,256]{1,0:T(8,128)(2,1)S(1)}, u32[]{:S(2)}, u32[]{:S(2)}) collective-permute-start(bf16[256,256]{1,0:T(8,128)(2,1)S(1)} %collective-permute-done.3.refs_2_), channel_id=1, source_target_pairs={{0,2},{1,3},{2,0},{3,1},{4,6},{5,7},{6,4},{7,5},{8,10},{9,11},{10,... | collective-permute-start | bytes 393224 | tf_op jit(solution)/shard_map/ppermute | solution.py:338
  80.5 2.9 %absorb.12.refs_4_ = f32[2,2,144,256]{3,2,1,0:T(8,128)S(1)} custom-call(bf16[384,256]{1,0:T(8,128)(2,1)S(1)} %collective-permute-done.refs_0_, bf16[384,256]{1,0:T(8,128)(2,1)S(1)} %collective-permute-done.1.refs_1_, bf16[512,256]{1,0:T(8,128)(2,1)S(1)} %collective-permute-done.21.refs_2_, bf16[512,256]{1,0:T(8,128)(2,1)S(1)} %collective-permute-done.16.refs_3_, ...), custom_call_target="tpu_custom_call" | custom-call | flops 536870912 | bytes 786432 | tf_op jit(solution)/shard_map/absorb/pallas_call | solution.py:184
  83.4 1.8 %absorb.13.refs_3_ = f32[2,2,144,256]{3,2,1,0:T(8,128)S(1)} custom-call(bf16[384,256]{1,0:T(8,128)(2,1)S(1)} %collective-permute-done.refs_0_, bf16[384,256]{1,0:T(8,128)(2,1)S(1)} %collective-permute-done.1.refs_1_, bf16[512,256]{1,0:T(8,128)(2,1)S(1)} %collective-permute-done.19.refs_2_, ...), custom_call_target="tpu_custom_call", output_to_operand_aliasing={{}: (4, {})} | custom-call | flops 268435456 | bytes 786432 | tf_op jit(solution)/shard_map/absorb/pallas_call | solution.py:184
  85.2 1.3 %absorb.14.refs_3_ = f32[2,2,144,256]{3,2,1,0:T(8,128)S(1)} custom-call(bf16[384,256]{1,0:T(8,128)(2,1)S(1)} %collective-permute-done.refs_0_, bf16[384,256]{1,0:T(8,128)(2,1)S(1)} %collective-permute-done.1.refs_1_, bf16[512,256]{1,0:T(8,128)(2,1)S(1)} %collective-permute-done.17.refs_2_, ...), custom_call_target="tpu_custom_call", output_to_operand_aliasing={{}: (3, {})} | custom-call | flops 134217728 | bytes 786432 | tf_op jit(solution)/shard_map/absorb/pallas_call | solution.py:184
  86.5 1.4 %absorb.15 = (bf16[256,256]{1,0:T(8,128)(2,1)S(1)}, bf16[256,256]{1,0:T(8,128)(2,1)S(1)}) custom-call(bf16[384,256]{1,0:T(8,128)(2,1)S(1)} %collective-permute-done.refs_0_, bf16[384,256]{1,0:T(8,128)(2,1)S(1)} %collective-permute-done.1.refs_1_, bf16[512,256]{1,0:T(8,128)(2,1)S(1)} %collective-permute-done.18.refs_2_, f32[2,2,144,256]{3,2,1,0:T(8,128)S(1)} %absorb.14.refs_3_), custom_call_target="tpu_custom_call" | custom-call | flops 134217728 | bytes 786432 | tf_op jit(solution)/shard_map/absorb/pallas_call | solution.py:184
  87.9 1.6 %collective-permute-start.24 = (bf16[256,256]{1,0:T(8,128)(2,1)S(1)}, bf16[256,256]{1,0:T(8,128)(2,1)S(1)}, u32[]{:S(2)}, u32[]{:S(2)}) collective-permute-start(bf16[256,256]{1,0:T(8,128)(2,1)S(1)} %get-tuple-element.27.ours), channel_id=1, source_target_pairs={{0,1},{1,0},{2,3},{3,2},{4,5},{5,4},{6,7},{7,6},{8,9},{9,8},{10,11... | collective-permute-start | bytes 393224 | tf_op jit(solution)/shard_map/ppermute | solution.py:338
  89.5 3.4 %collective-permute-done.27.back = bf16[256,256]{1,0:T(8,128)(2,1)S(1)} collective-permute-done((bf16[256,256]{1,0:T(8,128)(2,1)S(1)}, bf16[256,256]{1,0:T(8,128)(2,1)S(1)}, u32[]{:S(2)}, u32[]{:S(2)}) %collective-permute-start.27) | collective-permute-done | bytes 131104 | tf_op jit(solution)/shard_map/ppermute | solution.py:338
  92.9 1.0 collective-permute-start.25
  93.8 1.5 %absorb.8.refs_4_ = f32[1,2,144,256]{3,2,1,0:T(8,128)S(1)} custom-call(bf16[384,256]{1,0:T(8,128)(2,1)S(1)} %collective-permute-done.refs_0_, bf16[384,256]{1,0:T(8,128)(2,1)S(1)} %collective-permute-done.1.refs_1_, bf16[256,256]{1,0:T(8,128)(2,1)S(1)} %collective-permute-done.7.refs_2_, bf16[256,256]{1,0:T(8,128)(2,1)S(1)} %collective-permute-done.2.refs_3_, ...), custom_call_target="tpu_custom_call" | custom-call | flops 268435456 | bytes 393216 | tf_op jit(solution)/shard_map/absorb/pallas_call | solution.py:184
  95.3 1.0 absorb.9.refs_3_
  96.3 0.7 absorb.10.refs_3_
  97.0 0.8 absorb.11
  97.8 2.1 %collective-permute-start.10 = (bf16[256,128]{1,0:T(8,128)(2,1)S(1)}, bf16[256,128]{1,0:T(8,128)(2,1)S(1)}, u32[]{:S(2)}, u32[]{:S(2)}) collective-permute-start(bf16[256,128]{1,0:T(8,128)(2,1)S(1)} %get-tuple-element.22), channel_id=1, source_target_pairs={{0,4},{1,5},{2,6},{3,7},{4,0},{5,1},{6,2},{7,3},{8,12},{9,13},{10,... | collective-permute-start | bytes 196616 | tf_op jit(solution)/shard_map/ppermute | solution.py:338
  100.0 1.5 %collective-permute-start.11 = (bf16[256,128]{1,0:T(8,128)(2,1)S(1)}, bf16[256,128]{1,0:T(8,128)(2,1)S(1)}, u32[]{:S(2)}, u32[]{:S(2)}) collective-permute-start(bf16[256,128]{1,0:T(8,128)(2,1)S(1)} %get-tuple-element.23.third), channel_id=1, source_target_pairs={{0,1},{1,0},{2,3},{3,2},{4,5},{5,4},{6,7},{7,6},{8,9},{9,8},{10,11... | collective-permute-start | bytes 196616 | tf_op jit(solution)/shard_map/ppermute | solution.py:338
  101.5 1.3 %first_base.1 = (f32[256,1536]{1,0:T(8,128)S(1)}, f32[1,1536]{1,0:T(1,128)S(1)}) custom-call(s32[2]{0:T(128)S(1)} %get-tuple-element.32.spot_ref, bf16[256,256]{1,0:T(8,128)(2,1)S(1)} %get-tuple-element.27.ours, bf16[256,128]{1,0:T(8,128)(2,1)S(1)} %get-tuple-element.23.third, bf16[256,256]{1,0:T(8,128)(2,1)S(1)} %collective-permute-done.27.back, ...), custom_call_target="tpu_custom_call" | custom-call | flops 503316480 | bytes 1572864 | tf_op jit(solution)/shard_map/first_base/pallas_call | solution.py:214
  102.8 0.6 middle.1.refs_6_
  103.5 0.8 collective-permute-done.11.refs_1_
  104.3 0.8 collective-permute-done.12.refs_2_
  105.1 1.3 %finish.1 = bf16[256,1536]{1,0:T(8,128)(2,1)} custom-call(bf16[256,128]{1,0:T(8,128)(2,1)S(1)} %collective-permute-done.10.refs_0_, bf16[256,128]{1,0:T(8,128)(2,1)S(1)} %collective-permute-done.11.refs_1_, bf16[256,128]{1,0:T(8,128)(2,1)S(1)} %collective-permute-done.12.refs_2_, bf16[768,1536]{1,0:T(8,128)(2,1)S(1)} %collective-permute-done.13.weight.refs_3_, ...), custom_call_target="tpu_custom_call" | custom-call | flops 301989888 | bytes 786432 | tf_op jit(solution)/shard_map/finish/pallas_call | solution.py:283
  (31 shorter events, 1.7 us)
Async XLA Ops:
  3.9 96.1 %collective-permute-start.13 = (bf16[768,1536]{1,0:T(8,128)(2,1)}, bf16[768,1536]{1,0:T(8,128)(2,1)S(1)}, u32[]{:S(2)}, u32[]{:S(2)}) collective-permute-start(bf16[768,1536]{1,0:T(8,128)(2,1)} %carve.3), channel_id=1, source_target_pairs={{0,16},{1,17},{2,18},{3,19},{4,20},{5,21},{6,22},{7,23},{8,24},{9,... | collective-permute-start | bytes 7077896 | tf_op jit(solution)/shard_map/ppermute | solution.py:338
  4.5 5.3 %copy-start = (f32[1,3072]{1,0:T(1,128)S(1)}, f32[1,3072]{1,0:T(1,128)}, u32[]{:S(2)}) copy-start(f32[1,3072]{1,0:T(1,128)} %param.12) | copy-start | bytes 36868
  6.5 6.6 %collective-permute-start.2 = (bf16[256,256]{1,0:T(8,128)(2,1)S(1)}, bf16[256,256]{1,0:T(8,128)(2,1)S(1)}, u32[]{:S(2)}, u32[]{:S(2)}) collective-permute-start(bf16[256,256]{1,0:T(8,128)(2,1)S(1)} %get-tuple-element.20), channel_id=1, source_target_pairs={{0,20},{1,21},{2,22},{3,23},{4,16},{5,17},{6,18},{7,19},{8,28},{9,... | collective-permute-start | bytes 393224 | tf_op jit(solution)/shard_map/ppermute | solution.py:338
  9.3 6.1 %collective-permute-start.7 = (bf16[256,256]{1,0:T(8,128)(2,1)S(1)}, bf16[256,256]{1,0:T(8,128)(2,1)S(1)}, u32[]{:S(2)}, u32[]{:S(2)}) collective-permute-start(bf16[256,256]{1,0:T(8,128)(2,1)S(1)} %get-tuple-element.21), channel_id=1, source_target_pairs={{0,16},{1,17},{2,18},{3,19},{4,20},{5,21},{6,22},{7,23},{8,24},{9,... | collective-permute-start | bytes 393224 | tf_op jit(solution)/shard_map/ppermute | solution.py:338
  9.3 13.3 %collective-permute-start = (bf16[384,256]{1,0:T(8,128)(2,1)S(1)}, bf16[384,256]{1,0:T(8,128)(2,1)S(1)}, u32[]{:S(2)}, u32[]{:S(2)}) collective-permute-start(bf16[384,256]{1,0:T(8,128)(2,1)S(1)} %get-tuple-element.18), channel_id=1, source_target_pairs={{0,16},{1,17},{2,18},{3,19},{4,20},{5,21},{6,22},{7,23},{8,24},{9,... | collective-permute-start | bytes 589832 | tf_op jit(solution)/shard_map/ppermute | solution.py:338
  9.8 1.2 %collective-permute-start.29 = (f32[1,3072]{1,0:T(1,128)S(1)}, f32[1,3072]{1,0:T(1,128)S(1)}, u32[]{:S(2)}, u32[]{:S(2)}) collective-permute-start(f32[1,3072]{1,0:T(1,128)S(1)} %copy-done), channel_id=1, source_target_pairs={{0,16},{1,17},{2,18},{3,19},{4,20},{5,21},{6,22},{7,23},{8,24},{9,... | collective-permute-start | bytes 36872 | tf_op jit(solution)/shard_map/ppermute | solution.py:338
  10.9 5.6 %collective-permute-start.8 = (bf16[256,256]{1,0:T(8,128)(2,1)S(1)}, bf16[256,256]{1,0:T(8,128)(2,1)S(1)}, u32[]{:S(2)}, u32[]{:S(2)}) collective-permute-start(bf16[256,256]{1,0:T(8,128)(2,1)S(1)} %get-tuple-element.21), channel_id=1, source_target_pairs={{0,18},{1,19},{2,16},{3,17},{4,22},{5,23},{6,20},{7,21},{8,26},{9,... | collective-permute-start | bytes 393224 | tf_op jit(solution)/shard_map/ppermute | solution.py:338
  13.1 9.3 %collective-permute-start.5 = (bf16[256,256]{1,0:T(8,128)(2,1)S(1)}, bf16[256,256]{1,0:T(8,128)(2,1)S(1)}, u32[]{:S(2)}, u32[]{:S(2)}) collective-permute-start(bf16[256,256]{1,0:T(8,128)(2,1)S(1)} %get-tuple-element.21), channel_id=1, source_target_pairs={{0,24},{1,25},{2,26},{3,27},{4,28},{5,29},{6,30},{7,31},{8,16},{9,... | collective-permute-start | bytes 393224 | tf_op jit(solution)/shard_map/ppermute | solution.py:338
  15.4 9.1 %collective-permute-start.1 = (bf16[384,256]{1,0:T(8,128)(2,1)S(1)}, bf16[384,256]{1,0:T(8,128)(2,1)S(1)}, u32[]{:S(2)}, u32[]{:S(2)}) collective-permute-start(bf16[384,256]{1,0:T(8,128)(2,1)S(1)} %get-tuple-element.19), channel_id=1, source_target_pairs={{0,20},{1,21},{2,22},{3,23},{4,16},{5,17},{6,18},{7,19},{8,28},{9,... | collective-permute-start | bytes 589832 | tf_op jit(solution)/shard_map/ppermute | solution.py:338
  16.6 15.5 %collective-permute-start.16 = (bf16[512,256]{1,0:T(8,128)(2,1)S(1)}, bf16[512,256]{1,0:T(8,128)(2,1)S(1)}, u32[]{:S(2)}, u32[]{:S(2)}) collective-permute-start(bf16[512,256]{1,0:T(8,128)(2,1)S(1)} %get-tuple-element.25), channel_id=1, source_target_pairs={{0,20},{1,21},{2,22},{3,23},{4,16},{5,17},{6,18},{7,19},{8,28},{9,... | collective-permute-start | bytes 786440 | tf_op jit(solution)/shard_map/ppermute | solution.py:338
  22.4 11.2 %collective-permute-start.21 = (bf16[512,256]{1,0:T(8,128)(2,1)S(1)}, bf16[512,256]{1,0:T(8,128)(2,1)S(1)}, u32[]{:S(2)}, u32[]{:S(2)}) collective-permute-start(bf16[512,256]{1,0:T(8,128)(2,1)S(1)} %get-tuple-element.26), channel_id=1, source_target_pairs={{0,16},{1,17},{2,18},{3,19},{4,20},{5,21},{6,22},{7,23},{8,24},{9,... | collective-permute-start | bytes 786440 | tf_op jit(solution)/shard_map/ppermute | solution.py:338
  22.5 11.6 %collective-permute-start.22 = (bf16[512,256]{1,0:T(8,128)(2,1)S(1)}, bf16[512,256]{1,0:T(8,128)(2,1)S(1)}, u32[]{:S(2)}, u32[]{:S(2)}) collective-permute-start(bf16[512,256]{1,0:T(8,128)(2,1)S(1)} %get-tuple-element.26), channel_id=1, source_target_pairs={{0,18},{1,19},{2,16},{3,17},{4,22},{5,23},{6,20},{7,21},{8,26},{9,... | collective-permute-start | bytes 786440 | tf_op jit(solution)/shard_map/ppermute | solution.py:338
  24.5 17.3 %collective-permute-start.19 = (bf16[512,256]{1,0:T(8,128)(2,1)S(1)}, bf16[512,256]{1,0:T(8,128)(2,1)S(1)}, u32[]{:S(2)}, u32[]{:S(2)}) collective-permute-start(bf16[512,256]{1,0:T(8,128)(2,1)S(1)} %get-tuple-element.26), channel_id=1, source_target_pairs={{0,24},{1,25},{2,26},{3,27},{4,28},{5,29},{6,30},{7,31},{8,16},{9,... | collective-permute-start | bytes 786440 | tf_op jit(solution)/shard_map/ppermute | solution.py:338
  32.1 10.8 %collective-permute-start.9 = (bf16[256,256]{1,0:T(8,128)(2,1)S(1)}, bf16[256,256]{1,0:T(8,128)(2,1)S(1)}, u32[]{:S(2)}, u32[]{:S(2)}) collective-permute-start(bf16[256,256]{1,0:T(8,128)(2,1)S(1)} %collective-permute-done.2.refs_3_), channel_id=1, source_target_pairs={{0,2},{1,3},{2,0},{3,1},{4,6},{5,7},{6,4},{7,5},{8,10},{9,11},{10,... | collective-permute-start | bytes 393224 | tf_op jit(solution)/shard_map/ppermute | solution.py:338
  33.6 10.2 %collective-permute-start.6 = (bf16[256,256]{1,0:T(8,128)(2,1)S(1)}, bf16[256,256]{1,0:T(8,128)(2,1)S(1)}, u32[]{:S(2)}, u32[]{:S(2)}) collective-permute-start(bf16[256,256]{1,0:T(8,128)(2,1)S(1)} %collective-permute-done.5.refs_2_), channel_id=1, source_target_pairs={{0,2},{1,3},{2,0},{3,1},{4,6},{5,7},{6,4},{7,5},{8,10},{9,11},{10,... | collective-permute-start | bytes 393224 | tf_op jit(solution)/shard_map/ppermute | solution.py:338
  34.2 13.0 %collective-permute-start.3 = (bf16[256,256]{1,0:T(8,128)(2,1)S(1)}, bf16[256,256]{1,0:T(8,128)(2,1)S(1)}, u32[]{:S(2)}, u32[]{:S(2)}) collective-permute-start(bf16[256,256]{1,0:T(8,128)(2,1)S(1)} %collective-permute-done.2.refs_3_), channel_id=1, source_target_pairs={{0,8},{1,9},{2,10},{3,11},{4,12},{5,13},{6,14},{7,15},{8,0},{9,1},... | collective-permute-start | bytes 393224 | tf_op jit(solution)/shard_map/ppermute | solution.py:338
  41.7 9.0 %collective-permute-start.23 = (bf16[512,256]{1,0:T(8,128)(2,1)S(1)}, bf16[512,256]{1,0:T(8,128)(2,1)S(1)}, u32[]{:S(2)}, u32[]{:S(2)}) collective-permute-start(bf16[512,256]{1,0:T(8,128)(2,1)S(1)} %collective-permute-done.16.refs_3_), channel_id=1, source_target_pairs={{0,2},{1,3},{2,0},{3,1},{4,6},{5,7},{6,4},{7,5},{8,10},{9,11},{10,... | collective-permute-start | bytes 786440 | tf_op jit(solution)/shard_map/ppermute | solution.py:338
  42.9 13.4 %collective-permute-start.20 = (bf16[512,256]{1,0:T(8,128)(2,1)S(1)}, bf16[512,256]{1,0:T(8,128)(2,1)S(1)}, u32[]{:S(2)}, u32[]{:S(2)}) collective-permute-start(bf16[512,256]{1,0:T(8,128)(2,1)S(1)} %collective-permute-done.19.refs_2_), channel_id=1, source_target_pairs={{0,2},{1,3},{2,0},{3,1},{4,6},{5,7},{6,4},{7,5},{8,10},{9,11},{10,... | collective-permute-start | bytes 786440 | tf_op jit(solution)/shard_map/ppermute | solution.py:338
  43.8 28.4 %collective-permute-start.14 = (bf16[192,1536]{1,0:T(8,128)(2,1)S(1)}, bf16[192,1536]{1,0:T(8,128)(2,1)S(1)}, u32[]{:S(2)}, u32[]{:S(2)}) collective-permute-start(bf16[192,1536]{1,0:T(8,128)(2,1)S(1)} %get-tuple-element.24), channel_id=1, source_target_pairs={{0,17},{1,16},{2,19},{3,18},{4,21},{5,20},{6,23},{7,22},{8,25},{9,... | collective-permute-start | bytes 1769480 | tf_op jit(solution)/shard_map/ppermute | solution.py:338
  47.1 55.7 %collective-permute-start.26 = (bf16[384,1536]{1,0:T(8,128)(2,1)S(1)}, bf16[384,1536]{1,0:T(8,128)(2,1)S(1)}, u32[]{:S(2)}, u32[]{:S(2)}) collective-permute-start(bf16[384,1536]{1,0:T(8,128)(2,1)S(1)} %carve.4), channel_id=1, source_target_pairs={{0,17},{1,16},{2,19},{3,18},{4,21},{5,20},{6,23},{7,22},{8,25},{9,... | collective-permute-start | bytes 3538952 | tf_op jit(solution)/shard_map/ppermute | solution.py:338
  50.7 37.2 %collective-permute-start.28 = (bf16[256,1536]{1,0:T(8,128)(2,1)S(1)}, bf16[256,1536]{1,0:T(8,128)(2,1)S(1)}, u32[]{:S(2)}, u32[]{:S(2)}) collective-permute-start(bf16[256,1536]{1,0:T(8,128)(2,1)S(1)} %carve.5), channel_id=1, source_target_pairs={{0,16},{1,17},{2,18},{3,19},{4,20},{5,21},{6,22},{7,23},{8,24},{9,... | collective-permute-start | bytes 2359304 | tf_op jit(solution)/shard_map/ppermute | solution.py:338
  56.3 14.4 %collective-permute-start.17 = (bf16[512,256]{1,0:T(8,128)(2,1)S(1)}, bf16[512,256]{1,0:T(8,128)(2,1)S(1)}, u32[]{:S(2)}, u32[]{:S(2)}) collective-permute-start(bf16[512,256]{1,0:T(8,128)(2,1)S(1)} %collective-permute-done.16.refs_3_), channel_id=1, source_target_pairs={{0,8},{1,9},{2,10},{3,11},{4,12},{5,13},{6,14},{7,15},{8,0},{9,1},... | collective-permute-start | bytes 786440 | tf_op jit(solution)/shard_map/ppermute | solution.py:338
  70.7 8.3 %collective-permute-start.18 = (bf16[512,256]{1,0:T(8,128)(2,1)S(1)}, bf16[512,256]{1,0:T(8,128)(2,1)S(1)}, u32[]{:S(2)}, u32[]{:S(2)}) collective-permute-start(bf16[512,256]{1,0:T(8,128)(2,1)S(1)} %collective-permute-done.17.refs_2_), channel_id=1, source_target_pairs={{0,2},{1,3},{2,0},{3,1},{4,6},{5,7},{6,4},{7,5},{8,10},{9,11},{10,... | collective-permute-start | bytes 786440 | tf_op jit(solution)/shard_map/ppermute | solution.py:338
  72.2 30.6 %collective-permute-start.15 = (bf16[192,1536]{1,0:T(8,128)(2,1)S(1)}, bf16[192,1536]{1,0:T(8,128)(2,1)S(1)}, u32[]{:S(2)}, u32[]{:S(2)}) collective-permute-start(bf16[192,1536]{1,0:T(8,128)(2,1)S(1)} %collective-permute-done.14.passed.refs_4_), channel_id=1, source_target_pairs={{0,4},{1,5},{2,6},{3,7},{4,0},{5,1},{6,2},{7,3},{8,12},{9,13},{10,... | collective-permute-start | bytes 1769480 | tf_op jit(solution)/shard_map/ppermute | solution.py:338
  79.0 8.9 %collective-permute-start.4 = (bf16[256,256]{1,0:T(8,128)(2,1)S(1)}, bf16[256,256]{1,0:T(8,128)(2,1)S(1)}, u32[]{:S(2)}, u32[]{:S(2)}) collective-permute-start(bf16[256,256]{1,0:T(8,128)(2,1)S(1)} %collective-permute-done.3.refs_2_), channel_id=1, source_target_pairs={{0,2},{1,3},{2,0},{3,1},{4,6},{5,7},{6,4},{7,5},{8,10},{9,11},{10,... | collective-permute-start | bytes 393224 | tf_op jit(solution)/shard_map/ppermute | solution.py:338
  87.9 5.0 %collective-permute-start.27 = (bf16[256,256]{1,0:T(8,128)(2,1)S(1)}, bf16[256,256]{1,0:T(8,128)(2,1)S(1)}, u32[]{:S(2)}, u32[]{:S(2)}) collective-permute-start(bf16[256,256]{1,0:T(8,128)(2,1)S(1)} %get-tuple-element.28), channel_id=1, source_target_pairs={{0,4},{1,5},{2,6},{3,7},{4,0},{5,1},{6,2},{7,3},{8,12},{9,13},{10,... | collective-permute-start | bytes 393224 | tf_op jit(solution)/shard_map/ppermute | solution.py:338
  87.9 9.9 %collective-permute-start.24 = (bf16[256,256]{1,0:T(8,128)(2,1)S(1)}, bf16[256,256]{1,0:T(8,128)(2,1)S(1)}, u32[]{:S(2)}, u32[]{:S(2)}) collective-permute-start(bf16[256,256]{1,0:T(8,128)(2,1)S(1)} %get-tuple-element.27.ours), channel_id=1, source_target_pairs={{0,1},{1,0},{2,3},{3,2},{4,5},{5,4},{6,7},{7,6},{8,9},{9,8},{10,11... | collective-permute-start | bytes 393224 | tf_op jit(solution)/shard_map/ppermute | solution.py:338
  92.9 7.0 %collective-permute-start.25 = (bf16[256,256]{1,0:T(8,128)(2,1)S(1)}, bf16[256,256]{1,0:T(8,128)(2,1)S(1)}, u32[]{:S(2)}, u32[]{:S(2)}) collective-permute-start(bf16[256,256]{1,0:T(8,128)(2,1)S(1)} %get-tuple-element.28), channel_id=1, source_target_pairs={{0,5},{1,4},{2,7},{3,6},{4,1},{5,0},{6,3},{7,2},{8,13},{9,12},{10,... | collective-permute-start | bytes 393224 | tf_op jit(solution)/shard_map/ppermute | solution.py:338
  97.8 5.6 %collective-permute-start.10 = (bf16[256,128]{1,0:T(8,128)(2,1)S(1)}, bf16[256,128]{1,0:T(8,128)(2,1)S(1)}, u32[]{:S(2)}, u32[]{:S(2)}) collective-permute-start(bf16[256,128]{1,0:T(8,128)(2,1)S(1)} %get-tuple-element.22), channel_id=1, source_target_pairs={{0,4},{1,5},{2,6},{3,7},{4,0},{5,1},{6,2},{7,3},{8,12},{9,13},{10,... | collective-permute-start | bytes 196616 | tf_op jit(solution)/shard_map/ppermute | solution.py:338
  99.9 5.2 %collective-permute-start.12 = (bf16[256,128]{1,0:T(8,128)(2,1)S(1)}, bf16[256,128]{1,0:T(8,128)(2,1)S(1)}, u32[]{:S(2)}, u32[]{:S(2)}) collective-permute-start(bf16[256,128]{1,0:T(8,128)(2,1)S(1)} %get-tuple-element.22), channel_id=1, source_target_pairs={{0,5},{1,4},{2,7},{3,6},{4,1},{5,0},{6,3},{7,2},{8,13},{9,12},{10,... | collective-permute-start | bytes 196616 | tf_op jit(solution)/shard_map/ppermute | solution.py:338
  100.0 4.3 %collective-permute-start.11 = (bf16[256,128]{1,0:T(8,128)(2,1)S(1)}, bf16[256,128]{1,0:T(8,128)(2,1)S(1)}, u32[]{:S(2)}, u32[]{:S(2)}) collective-permute-start(bf16[256,128]{1,0:T(8,128)(2,1)S(1)} %get-tuple-element.23.third), channel_id=1, source_target_pairs={{0,1},{1,0},{2,3},{3,2},{4,5},{5,4},{6,7},{7,6},{8,9},{9,8},{10,11... | collective-permute-start | bytes 196616 | tf_op jit(solution)/shard_map/ppermute | solution.py:338
where the time goes:
time: 107 us; the launch traced here: 106 us
  waiting for transfers between devices  54.4 us (51%)
  starting transfers between devices  27.6 us (26%)
  Pallas kernels  24.1 us (23%)
    ppermute x30, waiting for transfers between devices, hop(): return lax.ppermute(block, ('segment', 'seq', 'head'), pairs)  54.4 us
    ppermute x30, starting transfers between devices, hop(): return lax.ppermute(block, ('segment', 'seq', 'head'), pairs)  27.6 us
    pallas_call x8, Pallas kernels, absorb(): pl.pallas_call(functools.partial(absorb_kernel, heads, len(blocks), first...  11.3 us
    pallas_call x3, Pallas kernels, carve(): pl.pallas_call(functools.partial(carve_kernel, local, cols, parts), out_s...  7.5 us
  transfers between devices with their start and end apart: 30, of which 13 were waited for; matrix products, arithmetic and copies ran while one was open for 0% of the time, Pallas kernels for 18%

commit v1 on v0

--- a/solution.py
+++ b/solution.py
@@ -11,7 +11,7 @@
 
 HD = 128
 STATE = HD + 16
-SHARED = 64
+SHARED = 32
 LOG2E = 1.4426950408889634
 VMEM = pl.BlockSpec(memory_space=pltpu.VMEM)
 
@@ -95,7 +95,7 @@
 def carve_kernel(local, cols, parts, spot_ref, w_any, *rest):
     out, sems = rest
     lanes = pl.ds(pl.multiple_of(spot_ref[1] * cols, HD), cols)
-    unit = HD // 2
+    unit = HD // 4
     copies, to = [], 0
     for ours, first, count in parts:
         role = spot_ref[0] if ours else 1 - spot_ref[0]
@@ -122,7 +122,7 @@
         out_shape=jax.ShapeDtypeStruct((rows, cols), weight.dtype),
         in_specs=[SMEM, ANY],
         out_specs=VMEM,
-        scratch_shapes=[pltpu.SemaphoreType.DMA((rows // (HD // 2),))],
+        scratch_shapes=[pltpu.SemaphoreType.DMA((rows // (HD // 4),))],
         compiler_params=limit(4),
         name="carve",
     )(spot, in_hbm(weight))
@@ -161,7 +161,7 @@
                 mixed = state[place, side, :HD, :] * shrink + mixed
                 total = state[place, side, HD : HD + 8, :] * shrink + total
             if last:
-                done = mixed * (1.0 / total[:1])
+                done = mixed / total[:1]
                 outs[side][:, place * HD : (place + 1) * HD] = done.T.astype(jnp.bfloat16)
             else:
                 outs[0][place, side, :HD, :] = mixed

time: 107 us -> 105 us (0.981)
  starting transfers between devices: 27.6 us -> 21.3 us
  waiting for transfers between devices: 54.4 us -> 58.7 us
    ppermute x30, starting transfers between devices: 27.6 us -> 21.3 us  [hop(): return lax.ppermute(block, ('segment', 'seq', 'head'), pairs)]
    ppermute x30, waiting for transfers between devices: 54.4 us -> 58.7 us  [hop(): return lax.ppermute(block, ('segment', 'seq', 'head'), pairs)]
  transfers between devices with their start and end apart: 30 -> 30, of which waited for: 13 -> 12; matrix products, arithmetic and copies ran while one was open for 0% -> 0% of each run, Pallas kernels for 18% -> 18%
where the time goes in v1:
time: 105 us
  waiting for transfers between devices  58.7 us (56%)
  Pallas kernels  24.4 us (23%)
  starting transfers between devices  21.3 us (20%)
    ppermute x30, waiting for transfers between devices, hop(): return lax.ppermute(block, ('segment', 'seq', 'head'), pairs)  58.7 us
    ppermute x30, starting transfers between devices, hop(): return lax.ppermute(block, ('segment', 'seq', 'head'), pairs)  21.3 us
    pallas_call x8, Pallas kernels, absorb(): pl.pallas_call(functools.partial(absorb_kernel, heads, len(blocks), first...  11.3 us
    pallas_call x3, Pallas kernels, carve(): pl.pallas_call(functools.partial(carve_kernel, local, cols, parts), out_s...  7.76 us
  transfers between devices with their start and end apart: 30, of which 12 were waited for; matrix products, arithmetic and copies ran while one was open for 0% of the time, Pallas kernels for 18%

profile of v1, /device:TPU:0, one launch (start us, length us, event | category | flops | bytes accessed | tf_op | source)
XLA Modules:
  0.0 104.7 jit_solution(4485780616593143596)
XLA Ops:
  0.0 0.1 iota_multiply_fusion
  0.1 3.9 %carve.3 = bf16[768,1536]{1,0:T(8,128)(2,1)} custom-call(s32[2]{0:T(128)S(1)} %get-tuple-element.32.spot_ref, bf16[768,3072]{1,0:T(8,128)(2,1)} %bitcast.9), custom_call_target="tpu_custom_call" | custom-call | tf_op jit(solution)/shard_map/carve/pallas_call | solution.py:120
  4.0 0.6 collective-permute-start.13
  4.6 2.0 %pack.1 = (bf16[512,256]{1,0:T(8,128)(2,1)S(1)}, bf16[256,256]{1,0:T(8,128)(2,1)S(1)}, bf16[512,256]{1,0:T(8,128)(2,1)S(1)}, bf16[256,256]{1,0:T(8,128)(2,1)S(1)...) custom-call(s32[2]{0:T(128)S(1)} %pad_add_fusion.spot_ref, ...), custom_call_target="tpu_custom_call" | custom-call | tf_op jit(solution)/shard_map/pack/pallas_call | solution.py:83
  6.6 2.7 %collective-permute-start.2 = (bf16[256,256]{1,0:T(8,128)(2,1)S(1)}, bf16[256,256]{1,0:T(8,128)(2,1)S(1)}, u32[]{:S(2)}, u32[]{:S(2)}) collective-permute-start(bf16[256,256]{1,0:T(8,128)(2,1)S(1)} %get-tuple-element.20), channel_id=1, source_target_pairs={{0,20},{1,21},{2,22},{3,23},{4,16},{5,17},{6,18},{7,19},{8,28},{9,... | collective-permute-start | bytes 393224 | tf_op jit(solution)/shard_map/ppermute | solution.py:338
  9.4 1.6 %collective-permute-start.8 = (bf16[256,256]{1,0:T(8,128)(2,1)S(1)}, bf16[256,256]{1,0:T(8,128)(2,1)S(1)}, u32[]{:S(2)}, u32[]{:S(2)}) collective-permute-start(bf16[256,256]{1,0:T(8,128)(2,1)S(1)} %get-tuple-element.21), channel_id=1, source_target_pairs={{0,18},{1,19},{2,16},{3,17},{4,22},{5,23},{6,20},{7,21},{8,26},{9,... | collective-permute-start | bytes 393224 | tf_op jit(solution)/shard_map/ppermute | solution.py:338
  11.0 1.2 %collective-permute-done.29.gate = f32[1,3072]{1,0:T(1,128)S(1)} collective-permute-done((f32[1,3072]{1,0:T(1,128)S(1)}, f32[1,3072]{1,0:T(1,128)S(1)}, u32[]{:S(2)}, u32[]{:S(2)}) %collective-permute-start.29) | collective-permute-done | bytes 12320 | tf_op jit(solution)/shard_map/ppermute | solution.py:338
  12.2 2.4 %collective-permute-start.5 = (bf16[256,256]{1,0:T(8,128)(2,1)S(1)}, bf16[256,256]{1,0:T(8,128)(2,1)S(1)}, u32[]{:S(2)}, u32[]{:S(2)}) collective-permute-start(bf16[256,256]{1,0:T(8,128)(2,1)S(1)} %get-tuple-element.21), channel_id=1, source_target_pairs={{0,24},{1,25},{2,26},{3,27},{4,28},{5,29},{6,30},{7,31},{8,16},{9,... | collective-permute-start | bytes 393224 | tf_op jit(solution)/shard_map/ppermute | solution.py:338
  14.5 0.3 collective-permute-start
  14.9 0.2 collective-permute-start.16
  15.1 1.5 %collective-permute-start.1 = (bf16[384,256]{1,0:T(8,128)(2,1)S(1)}, bf16[384,256]{1,0:T(8,128)(2,1)S(1)}, u32[]{:S(2)}, u32[]{:S(2)}) collective-permute-start(bf16[384,256]{1,0:T(8,128)(2,1)S(1)} %get-tuple-element.19), channel_id=1, source_target_pairs={{0,20},{1,21},{2,22},{3,23},{4,16},{5,17},{6,18},{7,19},{8,28},{9,... | collective-permute-start | bytes 589832 | tf_op jit(solution)/shard_map/ppermute | solution.py:338
  16.6 5.0 %collective-permute-done.5.refs_2_ = bf16[256,256]{1,0:T(8,128)(2,1)S(1)} collective-permute-done((bf16[256,256]{1,0:T(8,128)(2,1)S(1)}, bf16[256,256]{1,0:T(8,128)(2,1)S(1)}, u32[]{:S(2)}, u32[]{:S(2)}) %collective-permute-start.5) | collective-permute-done | bytes 131104 | tf_op jit(solution)/shard_map/ppermute | solution.py:338
  21.7 0.4 collective-permute-start.22
  22.1 7.9 %collective-permute-done.1.refs_1_ = bf16[384,256]{1,0:T(8,128)(2,1)S(1)} collective-permute-done((bf16[384,256]{1,0:T(8,128)(2,1)S(1)}, bf16[384,256]{1,0:T(8,128)(2,1)S(1)}, u32[]{:S(2)}, u32[]{:S(2)}) %collective-permute-start.1) | collective-permute-done | bytes 196640 | tf_op jit(solution)/shard_map/ppermute | solution.py:338
  30.0 1.3 %collective-permute-start.14 = (bf16[160,1536]{1,0:T(8,128)(2,1)S(1)}, bf16[160,1536]{1,0:T(8,128)(2,1)S(1)}, u32[]{:S(2)}, u32[]{:S(2)}) collective-permute-start(bf16[160,1536]{1,0:T(8,128)(2,1)S(1)} %get-tuple-element.24), channel_id=1, source_target_pairs={{0,17},{1,16},{2,19},{3,18},{4,21},{5,20},{6,23},{7,22},{8,25},{9,... | collective-permute-start | bytes 1474568 | tf_op jit(solution)/shard_map/ppermute | solution.py:338
  31.3 2.1 %carve.4 = bf16[448,1536]{1,0:T(8,128)(2,1)S(1)} custom-call(s32[2]{0:T(128)S(1)} %pad_add_fusion.spot_ref, bf16[768,3072]{1,0:T(8,128)(2,1)} %bitcast.11), custom_call_target="tpu_custom_call" | custom-call | tf_op jit(solution)/shard_map/carve/pallas_call | solution.py:120
  33.4 0.5 collective-permute-start.26
  34.0 1.1 %collective-permute-start.9 = (bf16[256,256]{1,0:T(8,128)(2,1)S(1)}, bf16[256,256]{1,0:T(8,128)(2,1)S(1)}, u32[]{:S(2)}, u32[]{:S(2)}) collective-permute-start(bf16[256,256]{1,0:T(8,128)(2,1)S(1)} %collective-permute-done.2.refs_3_), channel_id=1, source_target_pairs={{0,2},{1,3},{2,0},{3,1},{4,6},{5,7},{6,4},{7,5},{8,10},{9,11},{10,... | collective-permute-start | bytes 393224 | tf_op jit(solution)/shard_map/ppermute | solution.py:338
  35.1 10.8 %collective-permute-done.19.refs_2_ = bf16[512,256]{1,0:T(8,128)(2,1)S(1)} collective-permute-done((bf16[512,256]{1,0:T(8,128)(2,1)S(1)}, bf16[512,256]{1,0:T(8,128)(2,1)S(1)}, u32[]{:S(2)}, u32[]{:S(2)}) %collective-permute-start.19) | collective-permute-done | bytes 262176 | tf_op jit(solution)/shard_map/ppermute | solution.py:338
  45.9 0.2 collective-permute-start.6
  46.1 5.3 %collective-permute-done.6.refs_3_ = bf16[256,256]{1,0:T(8,128)(2,1)S(1)} collective-permute-done((bf16[256,256]{1,0:T(8,128)(2,1)S(1)}, bf16[256,256]{1,0:T(8,128)(2,1)S(1)}, u32[]{:S(2)}, u32[]{:S(2)}) %collective-permute-start.6) | collective-permute-done | bytes 131104 | tf_op jit(solution)/shard_map/ppermute | solution.py:338
  51.4 0.4 collective-permute-start.23
  51.8 1.8 %carve.5 = bf16[256,1536]{1,0:T(8,128)(2,1)S(1)} custom-call(s32[2]{0:T(128)S(1)} %get-tuple-element.31.spot_ref, bf16[256,3072]{1,0:T(8,128)(2,1)} %bitcast.12), custom_call_target="tpu_custom_call" | custom-call | tf_op jit(solution)/shard_map/carve/pallas_call | solution.py:120
  53.6 1.3 %collective-permute-done.3.refs_2_ = bf16[256,256]{1,0:T(8,128)(2,1)S(1)} collective-permute-done((bf16[256,256]{1,0:T(8,128)(2,1)S(1)}, bf16[256,256]{1,0:T(8,128)(2,1)S(1)}, u32[]{:S(2)}, u32[]{:S(2)}) %collective-permute-start.3) | collective-permute-done | bytes 131104 | tf_op jit(solution)/shard_map/ppermute | solution.py:338
  54.9 3.9 %collective-permute-done.23.refs_5_ = bf16[512,256]{1,0:T(8,128)(2,1)S(1)} collective-permute-done((bf16[512,256]{1,0:T(8,128)(2,1)S(1)}, bf16[512,256]{1,0:T(8,128)(2,1)S(1)}, u32[]{:S(2)}, u32[]{:S(2)}) %collective-permute-start.23) | collective-permute-done | bytes 262176 | tf_op jit(solution)/shard_map/ppermute | solution.py:338
  58.9 0.6 collective-permute-start.20
  59.5 9.5 %collective-permute-done.17.refs_2_ = bf16[512,256]{1,0:T(8,128)(2,1)S(1)} collective-permute-done((bf16[512,256]{1,0:T(8,128)(2,1)S(1)}, bf16[512,256]{1,0:T(8,128)(2,1)S(1)}, u32[]{:S(2)}, u32[]{:S(2)}) %collective-permute-start.17) | collective-permute-done | bytes 262176 | tf_op jit(solution)/shard_map/ppermute | solution.py:338
  69.0 1.6 %collective-permute-start.18 = (bf16[512,256]{1,0:T(8,128)(2,1)S(1)}, bf16[512,256]{1,0:T(8,128)(2,1)S(1)}, u32[]{:S(2)}, u32[]{:S(2)}) collective-permute-start(bf16[512,256]{1,0:T(8,128)(2,1)S(1)} %collective-permute-done.17.refs_2_), channel_id=1, source_target_pairs={{0,2},{1,3},{2,0},{3,1},{4,6},{5,7},{6,4},{7,5},{8,10},{9,11},{10,... | collective-permute-start | bytes 786440 | tf_op jit(solution)/shard_map/ppermute | solution.py:338
  70.6 6.6 %collective-permute-done.18.refs_2_ = bf16[512,256]{1,0:T(8,128)(2,1)S(1)} collective-permute-done((bf16[512,256]{1,0:T(8,128)(2,1)S(1)}, bf16[512,256]{1,0:T(8,128)(2,1)S(1)}, u32[]{:S(2)}, u32[]{:S(2)}) %collective-permute-start.18) | collective-permute-done | bytes 262176 | tf_op jit(solution)/shard_map/ppermute | solution.py:338
  77.3 1.6 %collective-permute-start.4 = (bf16[256,256]{1,0:T(8,128)(2,1)S(1)}, bf16[256,256]{1,0:T(8,128)(2,1)S(1)}, u32[]{:S(2)}, u32[]{:S(2)}) collective-permute-start(bf16[256,256]{1,0:T(8,128)(2,1)S(1)} %collective-permute-done.3.refs_2_), channel_id=1, source_target_pairs={{0,2},{1,3},{2,0},{3,1},{4,6},{5,7},{6,4},{7,5},{8,10},{9,11},{10,... | collective-permute-start | bytes 393224 | tf_op jit(solution)/shard_map/ppermute | solution.py:338
  78.9 2.9 %absorb.12.refs_4_ = f32[2,2,144,256]{3,2,1,0:T(8,128)S(1)} custom-call(bf16[384,256]{1,0:T(8,128)(2,1)S(1)} %collective-permute-done.refs_0_, bf16[384,256]{1,0:T(8,128)(2,1)S(1)} %collective-permute-done.1.refs_1_, bf16[512,256]{1,0:T(8,128)(2,1)S(1)} %collective-permute-done.21.refs_2_, bf16[512,256]{1,0:T(8,128)(2,1)S(1)} %collective-permute-done.16.refs_3_, ...), custom_call_target="tpu_custom_call" | custom-call | flops 536870912 | bytes 786432 | tf_op jit(solution)/shard_map/absorb/pallas_call | solution.py:184
  81.9 1.8 %absorb.13.refs_3_ = f32[2,2,144,256]{3,2,1,0:T(8,128)S(1)} custom-call(bf16[384,256]{1,0:T(8,128)(2,1)S(1)} %collective-permute-done.refs_0_, bf16[384,256]{1,0:T(8,128)(2,1)S(1)} %collective-permute-done.1.refs_1_, bf16[512,256]{1,0:T(8,128)(2,1)S(1)} %collective-permute-done.19.refs_2_, ...), custom_call_target="tpu_custom_call", output_to_operand_aliasing={{}: (4, {})} | custom-call | flops 268435456 | bytes 786432 | tf_op jit(solution)/shard_map/absorb/pallas_call | solution.py:184
  83.7 1.3 %absorb.14.refs_3_ = f32[2,2,144,256]{3,2,1,0:T(8,128)S(1)} custom-call(bf16[384,256]{1,0:T(8,128)(2,1)S(1)} %collective-permute-done.refs_0_, bf16[384,256]{1,0:T(8,128)(2,1)S(1)} %collective-permute-done.1.refs_1_, bf16[512,256]{1,0:T(8,128)(2,1)S(1)} %collective-permute-done.17.refs_2_, ...), custom_call_target="tpu_custom_call", output_to_operand_aliasing={{}: (3, {})} | custom-call | flops 134217728 | bytes 786432 | tf_op jit(solution)/shard_map/absorb/pallas_call | solution.py:184
  84.9 1.4 %absorb.15 = (bf16[256,256]{1,0:T(8,128)(2,1)S(1)}, bf16[256,256]{1,0:T(8,128)(2,1)S(1)}) custom-call(bf16[384,256]{1,0:T(8,128)(2,1)S(1)} %collective-permute-done.refs_0_, bf16[384,256]{1,0:T(8,128)(2,1)S(1)} %collective-permute-done.1.refs_1_, bf16[512,256]{1,0:T(8,128)(2,1)S(1)} %collective-permute-done.18.refs_2_, f32[2,2,144,256]{3,2,1,0:T(8,128)S(1)} %absorb.14.refs_3_), custom_call_target="tpu_custom_call" | custom-call | flops 134217728 | bytes 786432 | tf_op jit(solution)/shard_map/absorb/pallas_call | solution.py:184
  86.4 0.6 collective-permute-start.24
  87.0 4.4 %collective-permute-done.27.back = bf16[256,256]{1,0:T(8,128)(2,1)S(1)} collective-permute-done((bf16[256,256]{1,0:T(8,128)(2,1)S(1)}, bf16[256,256]{1,0:T(8,128)(2,1)S(1)}, u32[]{:S(2)}, u32[]{:S(2)}) %collective-permute-start.27) | collective-permute-done | bytes 131104 | tf_op jit(solution)/shard_map/ppermute | solution.py:338
  91.3 1.5 %absorb.8.refs_4_ = f32[1,2,144,256]{3,2,1,0:T(8,128)S(1)} custom-call(bf16[384,256]{1,0:T(8,128)(2,1)S(1)} %collective-permute-done.refs_0_, bf16[384,256]{1,0:T(8,128)(2,1)S(1)} %collective-permute-done.1.refs_1_, bf16[256,256]{1,0:T(8,128)(2,1)S(1)} %collective-permute-done.7.refs_2_, bf16[256,256]{1,0:T(8,128)(2,1)S(1)} %collective-permute-done.2.refs_3_, ...), custom_call_target="tpu_custom_call" | custom-call | flops 268435456 | bytes 393216 | tf_op jit(solution)/shard_map/absorb/pallas_call | solution.py:184
  92.8 1.0 absorb.9.refs_3_
  93.8 0.7 absorb.10.refs_3_
  94.5 0.8 absorb.11
  95.3 2.0 %collective-permute-start.10 = (bf16[256,128]{1,0:T(8,128)(2,1)S(1)}, bf16[256,128]{1,0:T(8,128)(2,1)S(1)}, u32[]{:S(2)}, u32[]{:S(2)}) collective-permute-start(bf16[256,128]{1,0:T(8,128)(2,1)S(1)} %get-tuple-element.22), channel_id=1, source_target_pairs={{0,4},{1,5},{2,6},{3,7},{4,0},{5,1},{6,2},{7,3},{8,12},{9,13},{10,... | collective-permute-start | bytes 196616 | tf_op jit(solution)/shard_map/ppermute | solution.py:338
  97.4 0.3 collective-permute-done.25.cross
  97.7 0.7 collective-permute-start.12
  98.4 0.5 collective-permute-start.11
  99.0 1.3 %first_base.1 = (f32[256,1536]{1,0:T(8,128)S(1)}, f32[1,1536]{1,0:T(1,128)S(1)}) custom-call(s32[2]{0:T(128)S(1)} %get-tuple-element.32.spot_ref, bf16[256,256]{1,0:T(8,128)(2,1)S(1)} %get-tuple-element.27.ours, bf16[256,128]{1,0:T(8,128)(2,1)S(1)} %get-tuple-element.23.third, bf16[256,256]{1,0:T(8,128)(2,1)S(1)} %collective-permute-done.27.back, ...), custom_call_target="tpu_custom_call" | custom-call | flops 503316480 | bytes 1572864 | tf_op jit(solution)/shard_map/first_base/pallas_call | solution.py:214
  100.3 0.6 middle.1.refs_6_
  101.0 2.4 %collective-permute-done.11.refs_1_ = bf16[256,128]{1,0:T(8,128)(2,1)S(1)} collective-permute-done((bf16[256,128]{1,0:T(8,128)(2,1)S(1)}, bf16[256,128]{1,0:T(8,128)(2,1)S(1)}, u32[]{:S(2)}, u32[]{:S(2)}) %collective-permute-start.11) | collective-permute-done | bytes 65568 | tf_op jit(solution)/shard_map/ppermute | solution.py:338
  103.4 1.4 %finish.1 = bf16[256,1536]{1,0:T(8,128)(2,1)} custom-call(bf16[256,128]{1,0:T(8,128)(2,1)S(1)} %collective-permute-done.10.refs_0_, bf16[256,128]{1,0:T(8,128)(2,1)S(1)} %collective-permute-done.11.refs_1_, bf16[256,128]{1,0:T(8,128)(2,1)S(1)} %collective-permute-done.12.refs_2_, bf16[768,1536]{1,0:T(8,128)(2,1)S(1)} %collective-permute-done.13.weight.refs_3_, ...), custom_call_target="tpu_custom_call" | custom-call | flops 301989888 | bytes 786432 | tf_op jit(solution)/shard_map/finish/pallas_call | solution.py:283
  (31 shorter events, 0.4 us)
Async XLA Ops:
  4.0 94.5 %collective-permute-start.13 = (bf16[768,1536]{1,0:T(8,128)(2,1)}, bf16[768,1536]{1,0:T(8,128)(2,1)S(1)}, u32[]{:S(2)}, u32[]{:S(2)}) collective-permute-start(bf16[768,1536]{1,0:T(8,128)(2,1)} %carve.3), channel_id=1, source_target_pairs={{0,16},{1,17},{2,18},{3,19},{4,20},{5,21},{6,22},{7,23},{8,24},{9,... | collective-permute-start | bytes 7077896 | tf_op jit(solution)/shard_map/ppermute | solution.py:338
  4.6 6.4 %copy-start = (f32[1,3072]{1,0:T(1,128)S(1)}, f32[1,3072]{1,0:T(1,128)}, u32[]{:S(2)}) copy-start(f32[1,3072]{1,0:T(1,128)} %param.12) | copy-start | bytes 36868
  6.6 7.9 %collective-permute-start.2 = (bf16[256,256]{1,0:T(8,128)(2,1)S(1)}, bf16[256,256]{1,0:T(8,128)(2,1)S(1)}, u32[]{:S(2)}, u32[]{:S(2)}) collective-permute-start(bf16[256,256]{1,0:T(8,128)(2,1)S(1)} %get-tuple-element.20), channel_id=1, source_target_pairs={{0,20},{1,21},{2,22},{3,23},{4,16},{5,17},{6,18},{7,19},{8,28},{9,... | collective-permute-start | bytes 393224 | tf_op jit(solution)/shard_map/ppermute | solution.py:338
  9.4 5.5 %collective-permute-start.7 = (bf16[256,256]{1,0:T(8,128)(2,1)S(1)}, bf16[256,256]{1,0:T(8,128)(2,1)S(1)}, u32[]{:S(2)}, u32[]{:S(2)}) collective-permute-start(bf16[256,256]{1,0:T(8,128)(2,1)S(1)} %get-tuple-element.21), channel_id=1, source_target_pairs={{0,16},{1,17},{2,18},{3,19},{4,20},{5,21},{6,22},{7,23},{8,24},{9,... | collective-permute-start | bytes 393224 | tf_op jit(solution)/shard_map/ppermute | solution.py:338
  9.4 5.7 %collective-permute-start.8 = (bf16[256,256]{1,0:T(8,128)(2,1)S(1)}, bf16[256,256]{1,0:T(8,128)(2,1)S(1)}, u32[]{:S(2)}, u32[]{:S(2)}) collective-permute-start(bf16[256,256]{1,0:T(8,128)(2,1)S(1)} %get-tuple-element.21), channel_id=1, source_target_pairs={{0,18},{1,19},{2,16},{3,17},{4,22},{5,23},{6,20},{7,21},{8,26},{9,... | collective-permute-start | bytes 393224 | tf_op jit(solution)/shard_map/ppermute | solution.py:338
  11.0 1.2 %collective-permute-start.29 = (f32[1,3072]{1,0:T(1,128)S(1)}, f32[1,3072]{1,0:T(1,128)S(1)}, u32[]{:S(2)}, u32[]{:S(2)}) collective-permute-start(f32[1,3072]{1,0:T(1,128)S(1)} %copy-done), channel_id=1, source_target_pairs={{0,16},{1,17},{2,18},{3,19},{4,20},{5,21},{6,22},{7,23},{8,24},{9,... | collective-permute-start | bytes 36872 | tf_op jit(solution)/shard_map/ppermute | solution.py:338
  12.2 9.5 %collective-permute-start.5 = (bf16[256,256]{1,0:T(8,128)(2,1)S(1)}, bf16[256,256]{1,0:T(8,128)(2,1)S(1)}, u32[]{:S(2)}, u32[]{:S(2)}) collective-permute-start(bf16[256,256]{1,0:T(8,128)(2,1)S(1)} %get-tuple-element.21), channel_id=1, source_target_pairs={{0,24},{1,25},{2,26},{3,27},{4,28},{5,29},{6,30},{7,31},{8,16},{9,... | collective-permute-start | bytes 393224 | tf_op jit(solution)/shard_map/ppermute | solution.py:338
  14.5 7.2 %collective-permute-start = (bf16[384,256]{1,0:T(8,128)(2,1)S(1)}, bf16[384,256]{1,0:T(8,128)(2,1)S(1)}, u32[]{:S(2)}, u32[]{:S(2)}) collective-permute-start(bf16[384,256]{1,0:T(8,128)(2,1)S(1)} %get-tuple-element.18), channel_id=1, source_target_pairs={{0,16},{1,17},{2,18},{3,19},{4,20},{5,21},{6,22},{7,23},{8,24},{9,... | collective-permute-start | bytes 589832 | tf_op jit(solution)/shard_map/ppermute | solution.py:338
  14.9 16.5 %collective-permute-start.16 = (bf16[512,256]{1,0:T(8,128)(2,1)S(1)}, bf16[512,256]{1,0:T(8,128)(2,1)S(1)}, u32[]{:S(2)}, u32[]{:S(2)}) collective-permute-start(bf16[512,256]{1,0:T(8,128)(2,1)S(1)} %get-tuple-element.25), channel_id=1, source_target_pairs={{0,20},{1,21},{2,22},{3,23},{4,16},{5,17},{6,18},{7,19},{8,28},{9,... | collective-permute-start | bytes 786440 | tf_op jit(solution)/shard_map/ppermute | solution.py:338
  15.1 15.0 %collective-permute-start.1 = (bf16[384,256]{1,0:T(8,128)(2,1)S(1)}, bf16[384,256]{1,0:T(8,128)(2,1)S(1)}, u32[]{:S(2)}, u32[]{:S(2)}) collective-permute-start(bf16[384,256]{1,0:T(8,128)(2,1)S(1)} %get-tuple-element.19), channel_id=1, source_target_pairs={{0,20},{1,21},{2,22},{3,23},{4,16},{5,17},{6,18},{7,19},{8,28},{9,... | collective-permute-start | bytes 589832 | tf_op jit(solution)/shard_map/ppermute | solution.py:338
  21.6 11.8 %collective-permute-start.21 = (bf16[512,256]{1,0:T(8,128)(2,1)S(1)}, bf16[512,256]{1,0:T(8,128)(2,1)S(1)}, u32[]{:S(2)}, u32[]{:S(2)}) collective-permute-start(bf16[512,256]{1,0:T(8,128)(2,1)S(1)} %get-tuple-element.26), channel_id=1, source_target_pairs={{0,16},{1,17},{2,18},{3,19},{4,20},{5,21},{6,22},{7,23},{8,24},{9,... | collective-permute-start | bytes 786440 | tf_op jit(solution)/shard_map/ppermute | solution.py:338
  21.7 12.3 %collective-permute-start.22 = (bf16[512,256]{1,0:T(8,128)(2,1)S(1)}, bf16[512,256]{1,0:T(8,128)(2,1)S(1)}, u32[]{:S(2)}, u32[]{:S(2)}) collective-permute-start(bf16[512,256]{1,0:T(8,128)(2,1)S(1)} %get-tuple-element.26), channel_id=1, source_target_pairs={{0,18},{1,19},{2,16},{3,17},{4,22},{5,23},{6,20},{7,21},{8,26},{9,... | collective-permute-start | bytes 786440 | tf_op jit(solution)/shard_map/ppermute | solution.py:338
  30.0 24.9 %collective-permute-start.14 = (bf16[160,1536]{1,0:T(8,128)(2,1)S(1)}, bf16[160,1536]{1,0:T(8,128)(2,1)S(1)}, u32[]{:S(2)}, u32[]{:S(2)}) collective-permute-start(bf16[160,1536]{1,0:T(8,128)(2,1)S(1)} %get-tuple-element.24), channel_id=1, source_target_pairs={{0,17},{1,16},{2,19},{3,18},{4,21},{5,20},{6,23},{7,22},{8,25},{9,... | collective-permute-start | bytes 1474568 | tf_op jit(solution)/shard_map/ppermute | solution.py:338
  31.3 14.5 %collective-permute-start.19 = (bf16[512,256]{1,0:T(8,128)(2,1)S(1)}, bf16[512,256]{1,0:T(8,128)(2,1)S(1)}, u32[]{:S(2)}, u32[]{:S(2)}) collective-permute-start(bf16[512,256]{1,0:T(8,128)(2,1)S(1)} %get-tuple-element.26), channel_id=1, source_target_pairs={{0,24},{1,25},{2,26},{3,27},{4,28},{5,29},{6,30},{7,31},{8,16},{9,... | collective-permute-start | bytes 786440 | tf_op jit(solution)/shard_map/ppermute | solution.py:338
  33.4 66.9 %collective-permute-start.26 = (bf16[448,1536]{1,0:T(8,128)(2,1)S(1)}, bf16[448,1536]{1,0:T(8,128)(2,1)S(1)}, u32[]{:S(2)}, u32[]{:S(2)}) collective-permute-start(bf16[448,1536]{1,0:T(8,128)(2,1)S(1)} %carve.4), channel_id=1, source_target_pairs={{0,17},{1,16},{2,19},{3,18},{4,21},{5,20},{6,23},{7,22},{8,25},{9,... | collective-permute-start | bytes 4128776 | tf_op jit(solution)/shard_map/ppermute | solution.py:338
  34.0 12.1 %collective-permute-start.9 = (bf16[256,256]{1,0:T(8,128)(2,1)S(1)}, bf16[256,256]{1,0:T(8,128)(2,1)S(1)}, u32[]{:S(2)}, u32[]{:S(2)}) collective-permute-start(bf16[256,256]{1,0:T(8,128)(2,1)S(1)} %collective-permute-done.2.refs_3_), channel_id=1, source_target_pairs={{0,2},{1,3},{2,0},{3,1},{4,6},{5,7},{6,4},{7,5},{8,10},{9,11},{10,... | collective-permute-start | bytes 393224 | tf_op jit(solution)/shard_map/ppermute | solution.py:338
  45.9 5.5 %collective-permute-start.6 = (bf16[256,256]{1,0:T(8,128)(2,1)S(1)}, bf16[256,256]{1,0:T(8,128)(2,1)S(1)}, u32[]{:S(2)}, u32[]{:S(2)}) collective-permute-start(bf16[256,256]{1,0:T(8,128)(2,1)S(1)} %collective-permute-done.5.refs_2_), channel_id=1, source_target_pairs={{0,2},{1,3},{2,0},{3,1},{4,6},{5,7},{6,4},{7,5},{8,10},{9,11},{10,... | collective-permute-start | bytes 393224 | tf_op jit(solution)/shard_map/ppermute | solution.py:338
  46.1 8.9 %collective-permute-start.3 = (bf16[256,256]{1,0:T(8,128)(2,1)S(1)}, bf16[256,256]{1,0:T(8,128)(2,1)S(1)}, u32[]{:S(2)}, u32[]{:S(2)}) collective-permute-start(bf16[256,256]{1,0:T(8,128)(2,1)S(1)} %collective-permute-done.2.refs_3_), channel_id=1, source_target_pairs={{0,8},{1,9},{2,10},{3,11},{4,12},{5,13},{6,14},{7,15},{8,0},{9,1},... | collective-permute-start | bytes 393224 | tf_op jit(solution)/shard_map/ppermute | solution.py:338
  51.4 7.5 %collective-permute-start.23 = (bf16[512,256]{1,0:T(8,128)(2,1)S(1)}, bf16[512,256]{1,0:T(8,128)(2,1)S(1)}, u32[]{:S(2)}, u32[]{:S(2)}) collective-permute-start(bf16[512,256]{1,0:T(8,128)(2,1)S(1)} %collective-permute-done.16.refs_3_), channel_id=1, source_target_pairs={{0,2},{1,3},{2,0},{3,1},{4,6},{5,7},{6,4},{7,5},{8,10},{9,11},{10,... | collective-permute-start | bytes 786440 | tf_op jit(solution)/shard_map/ppermute | solution.py:338
  54.9 31.5 %collective-permute-start.28 = (bf16[256,1536]{1,0:T(8,128)(2,1)S(1)}, bf16[256,1536]{1,0:T(8,128)(2,1)S(1)}, u32[]{:S(2)}, u32[]{:S(2)}) collective-permute-start(bf16[256,1536]{1,0:T(8,128)(2,1)S(1)} %carve.5), channel_id=1, source_target_pairs={{0,16},{1,17},{2,18},{3,19},{4,20},{5,21},{6,22},{7,23},{8,24},{9,... | collective-permute-start | bytes 2359304 | tf_op jit(solution)/shard_map/ppermute | solution.py:338
  54.9 14.1 %collective-permute-start.17 = (bf16[512,256]{1,0:T(8,128)(2,1)S(1)}, bf16[512,256]{1,0:T(8,128)(2,1)S(1)}, u32[]{:S(2)}, u32[]{:S(2)}) collective-permute-start(bf16[512,256]{1,0:T(8,128)(2,1)S(1)} %collective-permute-done.16.refs_3_), channel_id=1, source_target_pairs={{0,8},{1,9},{2,10},{3,11},{4,12},{5,13},{6,14},{7,15},{8,0},{9,1},... | collective-permute-start | bytes 786440 | tf_op jit(solution)/shard_map/ppermute | solution.py:338
  58.9 11.8 %collective-permute-start.20 = (bf16[512,256]{1,0:T(8,128)(2,1)S(1)}, bf16[512,256]{1,0:T(8,128)(2,1)S(1)}, u32[]{:S(2)}, u32[]{:S(2)}) collective-permute-start(bf16[512,256]{1,0:T(8,128)(2,1)S(1)} %collective-permute-done.19.refs_2_), channel_id=1, source_target_pairs={{0,2},{1,3},{2,0},{3,1},{4,6},{5,7},{6,4},{7,5},{8,10},{9,11},{10,... | collective-permute-start | bytes 786440 | tf_op jit(solution)/shard_map/ppermute | solution.py:338
  69.0 8.3 %collective-permute-start.18 = (bf16[512,256]{1,0:T(8,128)(2,1)S(1)}, bf16[512,256]{1,0:T(8,128)(2,1)S(1)}, u32[]{:S(2)}, u32[]{:S(2)}) collective-permute-start(bf16[512,256]{1,0:T(8,128)(2,1)S(1)} %collective-permute-done.17.refs_2_), channel_id=1, source_target_pairs={{0,2},{1,3},{2,0},{3,1},{4,6},{5,7},{6,4},{7,5},{8,10},{9,11},{10,... | collective-permute-start | bytes 786440 | tf_op jit(solution)/shard_map/ppermute | solution.py:338
  70.6 29.7 %collective-permute-start.15 = (bf16[160,1536]{1,0:T(8,128)(2,1)S(1)}, bf16[160,1536]{1,0:T(8,128)(2,1)S(1)}, u32[]{:S(2)}, u32[]{:S(2)}) collective-permute-start(bf16[160,1536]{1,0:T(8,128)(2,1)S(1)} %collective-permute-done.14.passed.refs_4_), channel_id=1, source_target_pairs={{0,4},{1,5},{2,6},{3,7},{4,0},{5,1},{6,2},{7,3},{8,12},{9,13},{10,... | collective-permute-start | bytes 1474568 | tf_op jit(solution)/shard_map/ppermute | solution.py:338
  77.3 9.0 %collective-permute-start.4 = (bf16[256,256]{1,0:T(8,128)(2,1)S(1)}, bf16[256,256]{1,0:T(8,128)(2,1)S(1)}, u32[]{:S(2)}, u32[]{:S(2)}) collective-permute-start(bf16[256,256]{1,0:T(8,128)(2,1)S(1)} %collective-permute-done.3.refs_2_), channel_id=1, source_target_pairs={{0,2},{1,3},{2,0},{3,1},{4,6},{5,7},{6,4},{7,5},{8,10},{9,11},{10,... | collective-permute-start | bytes 393224 | tf_op jit(solution)/shard_map/ppermute | solution.py:338
  86.3 5.0 %collective-permute-start.27 = (bf16[256,256]{1,0:T(8,128)(2,1)S(1)}, bf16[256,256]{1,0:T(8,128)(2,1)S(1)}, u32[]{:S(2)}, u32[]{:S(2)}) collective-permute-start(bf16[256,256]{1,0:T(8,128)(2,1)S(1)} %get-tuple-element.28), channel_id=1, source_target_pairs={{0,4},{1,5},{2,6},{3,7},{4,0},{5,1},{6,2},{7,3},{8,12},{9,13},{10,... | collective-permute-start | bytes 393224 | tf_op jit(solution)/shard_map/ppermute | solution.py:338
  86.4 8.9 %collective-permute-start.24 = (bf16[256,256]{1,0:T(8,128)(2,1)S(1)}, bf16[256,256]{1,0:T(8,128)(2,1)S(1)}, u32[]{:S(2)}, u32[]{:S(2)}) collective-permute-start(bf16[256,256]{1,0:T(8,128)(2,1)S(1)} %get-tuple-element.27.ours), channel_id=1, source_target_pairs={{0,1},{1,0},{2,3},{3,2},{4,5},{5,4},{6,7},{7,6},{8,9},{9,8},{10,11... | collective-permute-start | bytes 393224 | tf_op jit(solution)/shard_map/ppermute | solution.py:338
  91.3 6.4 %collective-permute-start.25 = (bf16[256,256]{1,0:T(8,128)(2,1)S(1)}, bf16[256,256]{1,0:T(8,128)(2,1)S(1)}, u32[]{:S(2)}, u32[]{:S(2)}) collective-permute-start(bf16[256,256]{1,0:T(8,128)(2,1)S(1)} %get-tuple-element.28), channel_id=1, source_target_pairs={{0,5},{1,4},{2,7},{3,6},{4,1},{5,0},{6,3},{7,2},{8,13},{9,12},{10,... | collective-permute-start | bytes 393224 | tf_op jit(solution)/shard_map/ppermute | solution.py:338
  95.3 5.6 %collective-permute-start.10 = (bf16[256,128]{1,0:T(8,128)(2,1)S(1)}, bf16[256,128]{1,0:T(8,128)(2,1)S(1)}, u32[]{:S(2)}, u32[]{:S(2)}) collective-permute-start(bf16[256,128]{1,0:T(8,128)(2,1)S(1)} %get-tuple-element.22), channel_id=1, source_target_pairs={{0,4},{1,5},{2,6},{3,7},{4,0},{5,1},{6,2},{7,3},{8,12},{9,13},{10,... | collective-permute-start | bytes 196616 | tf_op jit(solution)/shard_map/ppermute | solution.py:338
  97.7 5.7 %collective-permute-start.12 = (bf16[256,128]{1,0:T(8,128)(2,1)S(1)}, bf16[256,128]{1,0:T(8,128)(2,1)S(1)}, u32[]{:S(2)}, u32[]{:S(2)}) collective-permute-start(bf16[256,128]{1,0:T(8,128)(2,1)S(1)} %get-tuple-element.22), channel_id=1, source_target_pairs={{0,5},{1,4},{2,7},{3,6},{4,1},{5,0},{6,3},{7,2},{8,13},{9,12},{10,... | collective-permute-start | bytes 196616 | tf_op jit(solution)/shard_map/ppermute | solution.py:338
  98.4 5.0 %collective-permute-start.11 = (bf16[256,128]{1,0:T(8,128)(2,1)S(1)}, bf16[256,128]{1,0:T(8,128)(2,1)S(1)}, u32[]{:S(2)}, u32[]{:S(2)}) collective-permute-start(bf16[256,128]{1,0:T(8,128)(2,1)S(1)} %get-tuple-element.23.third), channel_id=1, source_target_pairs={{0,1},{1,0},{2,3},{3,2},{4,5},{5,4},{6,7},{7,6},{8,9},{9,8},{10,11... | collective-permute-start | bytes 196616 | tf_op jit(solution)/shard_map/ppermute | solution.py:338
